TPU v7x, 32 devices: a whole 2x2x4 slice. The times are simulated.
32 devices in a mesh: tm: 8 (over y, x, core), rows: 4 (over z).
Axes of the slice: x: 2, y: 2, z: 4, core: 2. Of those that a mesh axis runs over, the one named last changes fastest.
Arguments:
- frames_in: bfloat16 [32, 32, 32, 512], P('tm', 'rows'), may hold values from -6 to 6
- weight_in: bfloat16 [2, 512, 4608], P(None, 'rows'), may hold values from -0.09375 to 0.09375
- weight_out: bfloat16 [9, 2, 512, 512], P(None, None, 'rows'), may hold values from -0.015625 to 0.015625
- log_decay: float32 [512], replicated, may hold values from 0.0003125 to 0.06
- rotation: float32 [512], replicated, may hold values from -3.140625 to 3.140625
- start_state: float32 [32, 32, 2, 512], P('rows'), may hold values from -12 to 12
- skip_gain: float32 [512], replicated, may hold values from -1 to 1
Outputs:
- frames_out: bfloat16 [32, 32, 32, 512], P('tm', 'rows')
All inputs are finite; a program needn't handle non-finite values.
Results may differ from a plain program's by a relative error of at most 0.0047.
Values may be sent and summed in bfloat16 or wider, within the bound.
A program may use at most 128 MiB of HBM per device.

v0:
```python
import functools
import jax
import jax.numpy as jnp
from jax import lax
from jax.experimental import pallas as pl
from jax.experimental.pallas import tpu as pltpu
from jax.sharding import Mesh, PartitionSpec as P

CHIPS, CORE, ROWS = "chips", "core", "rows"


def shifted(value, axis, step):
    count = lax.axis_size(axis)
    pairs = [(i, i + step) for i in range(count) if 0 <= i + step < count]
    return lax.ppermute(value, axis, pairs)


def swapped(value):
    return lax.ppermute(value, CORE, [(0, 1), (1, 0)])


def with_halo(field):
    above = shifted(field[:, -1:], ROWS, 1)
    below = shifted(field[:, :1], ROWS, -1)
    return jnp.concatenate([above, field, below], axis=1)


def chip_at(place, chips):
    far = place // (chips // 2)
    return (1 - far) * (2 * place) + far * (2 * (chips - 1 - place) + 1)


def place_of(chip, chips):
    odd = chip % 2
    return (1 - odd) * (chip // 2) + odd * (chips - 1 - chip // 2)


def meet(chips, rows, chip, row, onward, back):
    barrier = pltpu.get_barrier_semaphore()

    def greet(**where):
        pl.semaphore_signal(
            barrier, inc=1, device_id=where, device_id_type=pl.DeviceIdType.MESH
        )

    greet(chips=onward)
    greet(chips=back)

    @pl.when(row > 0)
    def _():
        greet(rows=row - 1)

    @pl.when(row < rows - 1)
    def _():
        greet(rows=row + 1)

    sides = (row + rows - 1) // rows + (2 * rows - 2 - row) // rows
    pl.semaphore_wait(barrier, 2 + sides)


def spreader(leads, chips, rows, own_ref, full_ref, z_send, z_recv, r_send, r_recv, own_sem):
    chip, row = lax.axis_index(CHIPS), lax.axis_index(ROWS)
    place = place_of(chip, chips)
    onward = chip_at((place + 1) % chips, chips)
    back = chip_at((place + chips - 1) % chips, chips)
    many = chips // 2
    lead = (slice(None),) * leads

    def own_slice():
        return own_ref.at[lead + (chip // many, chip % many)]

    def block(shard, source, piece=None):
        at = lead + (source // many, shard, source % many)
        return full_ref.at[at if piece is None else at + (piece,)]

    keep = pltpu.make_async_copy(
        own_ref, full_ref.at[lead + (slice(None), row)], own_sem
    )

    def line(side, step):
        step_way = 1 - 2 * side
        shard = row - step_way * step
        src = own_slice() if step == 0 else block(shard, chip)
        return pltpu.make_async_remote_copy(
            src_ref=src,
            dst_ref=block(shard, chip),
            send_sem=z_send.at[side, step],
            recv_sem=z_recv.at[side, step],
            device_id={ROWS: row + step_way},
            device_id_type=pl.DeviceIdType.MESH,
        )

    def landed(side, step):
        shard = row - (1 - 2 * side) * (step + 1)
        here = block(shard, chip)
        return pltpu.make_async_remote_copy(
            src_ref=here,
            dst_ref=here,
            send_sem=z_send.at[side, step],
            recv_sem=z_recv.at[side, step],
            device_id={ROWS: row},
            device_id_type=pl.DeviceIdType.MESH,
        )

    def ring(side, step, way, turn):
        turn_way = 1 - 2 * way
        shard = row - (1 - 2 * side) * (step + 1)
        source = chip_at((place - turn_way * turn + chips) % chips, chips)
        here = block(shard, source, way)
        return pltpu.make_async_remote_copy(
            src_ref=here,
            dst_ref=here,
            send_sem=r_send.at[side, step, way, turn],
            recv_sem=r_recv.at[side, step, way, turn],
            device_id={CHIPS: back if way else onward},
            device_id_type=pl.DeviceIdType.MESH,
        )

    def ring_landed(side, step, way, turn):
        turn_way = 1 - 2 * way
        shard = row - (1 - 2 * side) * (step + 1)
        source = chip_at((place - turn_way * (turn + 1) + 2 * chips) % chips, chips)
        here = block(shard, source, way)
        return pltpu.make_async_remote_copy(
            src_ref=here,
            dst_ref=here,
            send_sem=r_send.at[side, step, way, turn],
            recv_sem=r_recv.at[side, step, way, turn],
            device_id={CHIPS: back if way else onward},
            device_id_type=pl.DeviceIdType.MESH,
        )

    def sends(side, step):
        near = row - step if side == 0 else rows - 1 - row - step
        room = rows - 1 - row if side == 0 else row
        return jnp.logical_and(near >= 0, room > 0)

    def comes(side, step):
        return (row if side == 0 else rows - 1 - row) > step

    def begin():
        keep.start()
        for side in range(2):

            @pl.when(sends(side, 0))
            def _():
                line(side, 0).start()

    def advance(tick):
        if tick < rows - 1:
            for side in range(2):

                @pl.when(comes(side, tick))
                def _():
                    landed(side, tick).wait_recv()
                    if tick + 1 < rows - 1:

                        @pl.when(sends(side, tick + 1))
                        def _():
                            line(side, tick + 1).start()

                    for way in range(2):
                        ring(side, tick, way, 0).start()

        for turn in range(1, chips):
            step = tick - turn
            if 0 <= step < rows - 1:
                for side in range(2):

                    @pl.when(comes(side, step))
                    def _():
                        for way in range(2):
                            ring_landed(side, step, way, turn - 1).wait_recv()
                            if turn < chips - 1:
                                ring(side, step, way, turn).start()

    def finish():
        for side in range(2):
            for step in range(rows - 1):

                @pl.when(sends(side, step))
                def _():
                    line(side, step).wait_send()

                @pl.when(comes(side, step))
                def _():
                    for way in range(2):
                        for turn in range(chips - 1):
                            ring(side, step, way, turn).wait_send()

    return begin, advance, finish, keep


def spread_kernel(leads, chips, rows, *refs):
    chip, row = lax.axis_index(CHIPS), lax.axis_index(ROWS)
    place = place_of(chip, chips)
    onward = chip_at((place + 1) % chips, chips)
    back = chip_at((place + chips - 1) % chips, chips)
    meet(chips, rows, chip, row, onward, back)
    begin, advance, finish, keep = spreader(leads, chips, rows, *refs)
    begin()
    for tick in range(rows - 1 + chips - 1):
        advance(tick)
    finish()
    keep.wait()


def semaphores(chips, rows):
    return [
        pltpu.SemaphoreType.DMA((2, rows - 1)),
        pltpu.SemaphoreType.DMA((2, rows - 1)),
        pltpu.SemaphoreType.DMA((2, rows - 1, 2, chips - 1)),
        pltpu.SemaphoreType.DMA((2, rows - 1, 2, chips - 1)),
        pltpu.SemaphoreType.DMA,
    ]


GROUPS = 4


def drive_kernel(chips, rows, in_ref, out_ref, field_ref, driven_ref, full_out, full_in, views, *sems):
    chip, row = lax.axis_index(CHIPS), lax.axis_index(ROWS)
    place = place_of(chip, chips)
    onward = chip_at((place + 1) % chips, chips)
    back = chip_at((place + chips - 1) % chips, chips)
    meet(chips, rows, chip, row, onward, back)
    count = len(sems) // 2
    first = spreader(0, chips, rows, in_ref, full_in, *sems[:count])
    second = spreader(1, chips, rows, out_ref, full_out, *sems[count:])
    ticks, delay = rows - 1 + chips - 1, rows - 1
    total, padded, columns, channels = field_ref.shape
    band = padded - 2
    group = total // GROUPS

    def compute(index):
        at = index * group
        taps = [
            views[b, at : at + group, a : a + band].reshape(group * band * columns, channels)
            for a in range(3)
            for b in range(3)
        ]
        window = jnp.concatenate(taps, axis=1)
        for part in range(2):
            weight = full_in[part]
            weight = weight.reshape(-1, weight.shape[-1])
            states = weight.shape[0]
            driven_ref[pl.ds(index * window.shape[0], window.shape[0]), part * states : (part + 1) * states] = (
                lax.dot_general(
                    window, weight, (((1,), (1,)), ((), ())), preferred_element_type=jnp.float32
                )
            )

    first[0]()

    @pl.loop(0, total)
    def _(frame):
        whole = field_ref[frame]
        wide = whole.astype(jnp.float32)
        edge = jnp.zeros((padded, 1, channels), jnp.float32)
        before = jnp.concatenate([edge, wide[:, : columns - 1]], axis=1)
        after = jnp.concatenate([wide[:, 1:], edge], axis=1)
        views[0, frame] = before.astype(whole.dtype)
        views[1, frame] = whole
        views[2, frame] = after.astype(whole.dtype)

    for tick in range(ticks):
        first[1](tick)
        if tick == delay - 1:
            second[0]()
        if tick >= delay:
            second[1](tick - delay)
    first[3].wait()
    for index in range(GROUPS):
        compute(index)
        if ticks - delay + index < ticks:
            second[1](ticks - delay + index)
    for tick in range(ticks - delay + GROUPS, ticks):
        second[1](tick)
    first[2]()
    second[2]()
    second[3].wait()


def drive(own_in, own_out, field, chips, rows):
    many_in = own_in.shape[:1] + (rows,) + own_in.shape[1:]
    many_out = own_out.shape[:2] + (rows,) + own_out.shape[2:]
    total, padded, columns, channels = field.shape
    pixels = total * (padded - 2) * columns
    states = many_in[1] * many_in[2] * many_in[3] * many_in[4]
    vmem = pl.BlockSpec(memory_space=pltpu.VMEM)
    return pl.pallas_call(
        functools.partial(drive_kernel, chips, rows),
        out_shape=(
            jax.ShapeDtypeStruct((pixels, 2 * states), jnp.float32),
            jax.ShapeDtypeStruct(many_out, own_out.dtype),
        ),
        in_specs=[vmem, vmem, vmem],
        out_specs=(vmem, pl.BlockSpec(memory_space=pl.ANY)),
        scratch_shapes=[
            pltpu.VMEM(many_in, own_in.dtype),
            pltpu.VMEM((3,) + field.shape, field.dtype),
        ]
        + semaphores(chips, rows)
        + semaphores(chips, rows),
        compiler_params=pltpu.CompilerParams(
            collective_id=2, has_side_effects=True, vmem_limit_bytes=60 * 1024 * 1024
        ),
    )(own_in, own_out, field)


def spread(own, leads, chips, rows, number):
    shape = own.shape[: leads + 1] + (rows,) + own.shape[leads + 1 :]
    any_space = pl.BlockSpec(memory_space=pl.ANY)
    return pl.pallas_call(
        functools.partial(spread_kernel, leads, chips, rows),
        out_shape=jax.ShapeDtypeStruct(shape, own.dtype),
        in_specs=[pl.BlockSpec(memory_space=pltpu.VMEM)],
        out_specs=any_space,
        scratch_shapes=semaphores(chips, rows),
        compiler_params=pltpu.CompilerParams(collective_id=number, has_side_effects=True),
    )(own)


def conv(field, weight, form):
    return lax.conv_general_dilated(
        field, weight, (1, 1), ((0, 0), (1, 1)),
        dimension_numbers=("NHWC", form, "NHWC"),
        preferred_element_type=jnp.float32,
    )


def recur_kernel(last_only, both_ref, begin_ref, factor_ref, result_ref):
    states = factor_ref.shape[1]
    lam_re, lam_im = factor_ref[0:1, :], factor_ref[1:2, :]
    state_re, state_im = begin_ref[0, :, :states], begin_ref[0, :, states:]
    total = both_ref.shape[0]
    for t in range(total):
        state_re, state_im = (
            lam_re * state_re - lam_im * state_im + both_ref[t, 0, :, :states],
            lam_re * state_im + lam_im * state_re + both_ref[t, 0, :, states:],
        )
        if not last_only:
            result_ref[t, 0, :, :states] = state_re.astype(result_ref.dtype)
            result_ref[t, 0, :, states:] = state_im.astype(result_ref.dtype)
    if last_only:
        result_ref[0, :, :states] = state_re.astype(result_ref.dtype)
        result_ref[0, :, states:] = state_im.astype(result_ref.dtype)


def recur(both, begin, factor, last_only):
    total, band, columns, lanes = both.shape
    frames = pl.BlockSpec((total, 1, columns, lanes), lambda i: (0, i, 0, 0))
    single = pl.BlockSpec((1, columns, lanes), lambda i: (i, 0, 0))
    shape = both.shape[1:] if last_only else both.shape
    return pl.pallas_call(
        functools.partial(recur_kernel, last_only),
        out_shape=jax.ShapeDtypeStruct(shape, jnp.bfloat16),
        grid=(band,),
        in_specs=[frames, single, pl.BlockSpec(factor.shape, lambda i: (0, 0))],
        out_specs=single if last_only else frames,
    )(both, begin, factor)


def powers(log_rate, angle, exponent):
    modulus = jnp.exp(-log_rate * exponent)
    return modulus * jnp.cos(angle * exponent), modulus * jnp.sin(angle * exponent)


def on_device(frames_in, weight_in, weight_out, log_decay, rotation, start_state, skip_gain):
    frame_count, band_rows, columns, channels = frames_in.shape
    shard = weight_in.shape[1]
    chips, cores, rows = (lax.axis_size(a) for a in (CHIPS, CORE, ROWS))
    core, chip = lax.axis_index(CORE), lax.axis_index(CHIPS)
    half = shard // cores
    many = chips // 2
    piece = half // (2 * many)

    def own(vector, axis):
        picks = [
            jnp.concatenate(
                [
                    lax.slice_in_dim(vector, r * shard + c * half, r * shard + (c + 1) * half, axis=axis)
                    for r in range(rows)
                ],
                axis=axis,
            )
            for c in range(cores)
        ]
        return jnp.where(core == 0, picks[0], picks[1])

    states = rows * half
    slice_in = lax.dynamic_slice_in_dim(weight_in, core * half, half, 1)
    slice_out = lax.dynamic_slice_in_dim(weight_out, core * half, half, 2)
    own_in = slice_in.reshape(2, many, 2, piece, 9 * channels)
    own_out = slice_out.reshape(9, 2, many, 2, piece, channels)

    mine = with_halo(frames_in)
    theirs = swapped(mine)
    first = jnp.where(core == 0, mine, theirs)
    second = jnp.where(core == 0, theirs, mine)
    field = jnp.concatenate([first, second], axis=0)
    total = field.shape[0]

    if piece % 16 == 0 and total % GROUPS == 0:
        both, out_full = drive(own_in, own_out, field, chips, rows)
        both = both.reshape(total, band_rows, columns, 2 * states)
    else:
        in_full = spread(own_in, 0, chips, rows, 0).reshape(2, states, 3, 3, channels)
        out_full = spread(own_out, 1, chips, rows, 1)
        both = jnp.concatenate(
            [conv(field, in_full[part], "OHWI") for part in range(2)], axis=-1
        )

    log_rate, angle = own(log_decay, 0), own(rotation, 0)
    start = own(start_state, 3)
    lam_re, lam_im = powers(log_rate, angle, jnp.float32(1.0))
    begin = jnp.concatenate([start[:, :, 0], start[:, :, 1]], axis=-1)
    begin = jnp.where(chip == 0, begin, jnp.float32(0.0))
    factor = jnp.stack([lam_re, lam_im])
    tail = recur(both, begin, factor, True)
    carry_re = carry_im = jnp.float32(0.0)
    for step in range(1, chips):
        far = shifted(tail, CHIPS, step).astype(jnp.float32)
        jump_re, jump_im = powers(log_rate, angle, jnp.float32(total * (step - 1)))
        carry_re = carry_re + jump_re * far[..., :states] - jump_im * far[..., states:]
        carry_im = carry_im + jump_re * far[..., states:] + jump_im * far[..., :states]
    begin = begin + jnp.concatenate([carry_re, carry_im], axis=-1)
    held = with_halo(recur(both, begin, factor, False))

    out_weight = out_full.reshape(3, 3, 2 * states, channels)
    held_theirs = lax.dynamic_slice_in_dim(held, (1 - core) * frame_count, frame_count, 0)
    held_mine = lax.dynamic_slice_in_dim(held, core * frame_count, frame_count, 0)
    sent = conv(held_theirs, out_weight, "HWIO").astype(jnp.bfloat16)
    got = swapped(sent).astype(jnp.float32)
    mixing = conv(held_mine, out_weight, "HWIO") + got
    pre_act = mixing + skip_gain * frames_in.astype(jnp.float32)
    return jax.nn.gelu(pre_act, approximate=False).astype(jnp.bfloat16)


def solution(mesh):
    count, rows = mesh.devices.shape
    fine = Mesh(mesh.devices.reshape(count // 2, 2, rows), (CHIPS, CORE, ROWS))
    frames = P((CHIPS, CORE), ROWS, None, None)
    return jax.shard_map(
        on_device,
        mesh=fine,
        in_specs=(
            frames,
            P(None, ROWS, None),
            P(None, None, ROWS, None),
            P(),
            P(),
            P(ROWS, None, None, None),
            P(),
        ),
        out_specs=frames,
        check_vma=False,
    )
```

profile of v0, /device:TPU:5, one launch (start us, length us, event | category | flops | bytes accessed | tf_op | source)
XLA Modules:
  0.0 179.9 jit_solution(11021136798846247144)
XLA Ops:
  0.0 1.8 %fusion.34 = (bf16[4,1,32,512]{3,2,1,0:T(8,128)(2,1)}, bf16[4,1,32,512]{3,2,1,0:T(8,128)(2,1)}) fusion(bf16[4,8,32,512]{3,2,1,0:T(8,128)(2,1)} %param.7), kind=kLoop, calls=%fused_computation.91 | loop fusion | bytes 524288 | tf_op jit(solution)/shard_map/slice | solution.py:24
  1.8 3.8 %collective-permute-start = (bf16[4,1,32,512]{3,2,1,0:T(8,128)(2,1)}, bf16[4,1,32,512]{3,2,1,0:T(8,128)(2,1)}, u32[]{:S(2)}, u32[]{:S(2)}) collective-permute-start(bf16[4,1,32,512]{3,2,1,0:T(8,128)(2,1)} %get-tuple-element.32), channel_id=1, source_target_pairs={{0,1},{1,2},{2,3},{4,5},{5,6},{6,7},{8,9},{9,10},{10,11},{12,13},{... | collective-permute-start | bytes 393224 | tf_op jit(solution)/shard_map/ppermute | solution.py:15
  5.7 1.3 collective-permute-start.1
  7.0 2.7 %fusion.33 = (f32[8,32,2,64]{3,2,1,0:T(2,128)S(1)}, f32[8,32,2,64]{3,2,1,0:T(2,128)S(1)}, f32[8,32,2,64]{3,2,1,0:T(2,128)S(1)}, f32[8,32,2,64]{3,2,1,0:T(2,128)S...) fusion(f32[8,32,2,512]{3,2,1,0:T(2,128)} %param.12), kind=kLoop, calls=%fused_computation.90 | loop fusion | bytes 2097152 | tf_op jit(solution)/shard_map/slice | solution.py:382
  23.2 1.2 constant_dynamic-slice_fusion.1
  24.6 1.7 pad_maximum_fusion.field_ref
  26.3 80.9 %shard_map.73 = (f32[2048,512]{1,0:T(8,128)}, bf16[9,2,4,2,2,16,512]{6,5,4,3,2,1,0:T(8,128)(2,1)}) custom-call(bf16[2,2,2,16,4608]{4,3,2,1,0:T(8,128)(2,1)} %bitcast.78, bf16[9,2,2,2,16,512]{5,4,3,2,1,0:T(8,128)(2,1)} %bitcast.77, bf16[8,10,32,512]{3,2,1,0:T(8,128)(2,1)} %pad_maximum_fusion.field_ref), custom_call_target="tpu_custom_call" | custom-call | tf_op jit(solution)/shard_map/pallas_call | solution.py:291
  107.4 5.9 %shard_map.74 = bf16[8,32,512]{2,1,0:T(8,128)(2,1)} custom-call(f32[8,8,32,512]{3,2,1,0:T(8,128)} %bitcast.70, f32[8,32,512]{2,1,0:T(8,128)} %maximum_select_fusion.1.begin_ref, f32[2,256]{1,0:T(2,128)} %pad_maximum_fusion.2.factor_ref), custom_call_target="tpu_custom_call" | custom-call | tf_op jit(solution)/shard_map/pallas_call | solution.py:355
  113.9 1.3 collective-permute-start.4
  115.2 3.7 %collective-permute-start.3 = (bf16[8,32,512]{2,1,0:T(8,128)(2,1)}, bf16[8,32,512]{2,1,0:T(8,128)(2,1)S(1)}, u32[]{:S(2)}, u32[]{:S(2)}) collective-permute-start(bf16[8,32,512]{2,1,0:T(8,128)(2,1)} %shard_map.74), channel_id=1, source_target_pairs={{0,8},{8,16},{16,24},{1,9},{9,17},{17,25},{2,10},{10,18},{18,26},{... | collective-permute-start | bytes 786440 | tf_op jit(solution)/shard_map/ppermute | solution.py:15
  119.4 9.9 %collective-permute-done.4 = bf16[8,32,512]{2,1,0:T(8,128)(2,1)S(1)} collective-permute-done((bf16[8,32,512]{2,1,0:T(8,128)(2,1)}, bf16[8,32,512]{2,1,0:T(8,128)(2,1)S(1)}, u32[]{:S(2)}, u32[]{:S(2)}) %collective-permute-start.4) | collective-permute-done | bytes 262176 | tf_op jit(solution)/shard_map/ppermute | solution.py:15
  130.5 6.3 %shard_map.75 = bf16[8,8,32,512]{3,2,1,0:T(8,128)(2,1)} custom-call(f32[8,8,32,512]{3,2,1,0:T(8,128)} %bitcast.71, f32[8,32,512]{2,1,0:T(8,128)} %maximum_add_fusion.begin_ref, f32[2,256]{1,0:T(2,128)} %pad_maximum_fusion.2.factor_ref), custom_call_target="tpu_custom_call" | custom-call | tf_op jit(solution)/shard_map/pallas_call | solution.py:355
  137.9 1.3 collective-permute-start.7
  139.2 4.0 %collective-permute-start.6 = (bf16[8,1,32,512]{3,2,1,0:T(8,128)(2,1)S(1)}, bf16[8,1,32,512]{3,2,1,0:T(8,128)(2,1)S(1)}, u32[]{:S(2)}, u32[]{:S(2)}) collective-permute-start(bf16[8,1,32,512]{3,2,1,0:T(8,128)(2,1)S(1)} %get-tuple-element.19), channel_id=1, source_target_pairs={{0,1},{1,2},{2,3},{4,5},{5,6},{6,7},{8,9},{9,10},{10,11},{12,13},{... | collective-permute-start | bytes 786440 | tf_op jit(solution)/shard_map/ppermute | solution.py:15
  143.2 1.8 %collective-permute-done.7 = bf16[8,1,32,512]{3,2,1,0:T(8,128)(2,1)S(1)} collective-permute-done((bf16[8,1,32,512]{3,2,1,0:T(8,128)(2,1)S(1)}, bf16[8,1,32,512]{3,2,1,0:T(8,128)(2,1)S(1)}, u32[]{:S(2)}, u32[]{:S(2)}) %collective-permute-start.7) | collective-permute-done | bytes 262176 | tf_op jit(solution)/shard_map/ppermute | solution.py:15
  145.0 1.5 collective-permute-done.6
  146.5 1.9 %pad_maximum_fusion.1 = bf16[8,10,32,512]{3,2,1,0:T(8,128)(2,1)S(1)} fusion(bf16[8,1,32,512]{3,2,1,0:T(8,128)(2,1)S(1)} %collective-permute-done.7, bf16[8,8,32,512]{3,2,1,0:T(8,128)(2,1)} %shard_map.75, bf16[8,1,32,512]{3,2,1,0:T(8,128)(2,1)S(1)} %collective-permute-done.6), kind=kLoop, calls=%fused_computation.5 | loop fusion | flops 2621440 | bytes 5242880 | tf_op jit(solution)/shard_map/concatenate | solution.py:25
  151.6 6.3 %select_convert_fusion = bf16[8,32,5,512]{3,1,2,0:T(8,128)(2,1)S(1)} fusion(bf16[3,3,512,512]{3,2,1,0:T(8,128)(2,1)S(1)} %bitcast.82, bf16[10,4,8,7,512]{4,1,3,2,0:T(4,128)(2,1)S(1)} %fusion.3, pred[32,5]{0,1:T(8,128)(4,1)S(1)} %copy-done.29), kind=kOutput, calls=%fused_computation.6 | convolution fusion | flops 6041108480 | bytes 8323232 | tf_op jit(solution)/shard_map/conv_general_dilated | solution.py:325
  158.7 3.6 %collective-permute-start.8 = (bf16[4,8,32,512]{3,1,2,0:T(8,128)(2,1)S(1)}, bf16[4,8,32,512]{3,1,2,0:T(8,128)(2,1)S(1)}, u32[]{:S(2)}, u32[]{:S(2)}) collective-permute-start(bf16[4,8,32,512]{3,1,2,0:T(8,128)(2,1)S(1)} %slice_bitcast_fusion.1), channel_id=1, source_target_pairs={{0,4},{4,0},{1,5},{5,1},{2,6},{6,2},{3,7},{7,3},{8,12},{12,8},{9,1... | collective-permute-start | bytes 3145736 | tf_op jit(solution)/shard_map/ppermute | solution.py:19
  164.2 1.3 fusion.2
  165.5 6.3 %fusion.22 = f32[8,32,5,512]{3,1,2,0:T(8,128)S(1)} fusion(bf16[3,3,512,512]{3,2,1,0:T(8,128)(2,1)S(1)} %bitcast.83, bf16[10,4,8,7,512]{4,1,3,2,0:T(4,128)(2,1)S(1)} %fusion.2, pred[32,5]{0,1:T(8,128)(4,1)S(1)} %copy-done.29), kind=kOutput, calls=%fused_computation.36 | convolution fusion | flops 6040453120 | bytes 9633952 | tf_op jit(solution)/shard_map/conv_general_dilated | solution.py:325
  171.8 1.5 copy.28
  173.4 5.2 %fusion.12 = bf16[4,8,32,512]{3,1,2,0:T(8,128)(2,1)S(1)} fusion(bf16[4,8,32,512]{3,1,2,0:T(8,128)(2,1)S(1)} %collective-permute-done.8, f32[8,4,40,512]{3,0,2,1:T(8,128)S(1)} %bitcast.76, bf16[4,8,32,512]{3,2,1,0:T(8,128)(2,1)S(1)} %copy-done.2, f32[512]{0:T(512)S(1)} %copy-done.15), kind=kLoop, calls=%fused_computation.17 | loop fusion | flops 36700160 | bytes 5244928 | tf_op jit(solution)/shard_map/convert_element_type | solution.py:437
  178.6 1.3 copy.33
  (112 shorter events, 22.6 us)
Async XLA Ops:
  0.0 22.1 %copy-start = (bf16[9,2,128,512]{3,2,1,0:T(8,128)(2,1)S(1)}, bf16[9,2,128,512]{3,2,1,0:T(8,128)(2,1)}, u32[]{:S(2)}) copy-start(bf16[9,2,128,512]{3,2,1,0:T(8,128)(2,1)} %param.9) | copy-start | bytes 7077892
  1.8 16.2 %collective-permute-start = (bf16[4,1,32,512]{3,2,1,0:T(8,128)(2,1)}, bf16[4,1,32,512]{3,2,1,0:T(8,128)(2,1)}, u32[]{:S(2)}, u32[]{:S(2)}) collective-permute-start(bf16[4,1,32,512]{3,2,1,0:T(8,128)(2,1)} %get-tuple-element.32), channel_id=1, source_target_pairs={{0,1},{1,2},{2,3},{4,5},{5,6},{6,7},{8,9},{9,10},{10,11},{12,13},{... | collective-permute-start | bytes 393224 | tf_op jit(solution)/shard_map/ppermute | solution.py:15
  5.7 13.3 %collective-permute-start.1 = (bf16[4,1,32,512]{3,2,1,0:T(8,128)(2,1)}, bf16[4,1,32,512]{3,2,1,0:T(8,128)(2,1)S(1)}, u32[]{:S(2)}, u32[]{:S(2)}) collective-permute-start(bf16[4,1,32,512]{3,2,1,0:T(8,128)(2,1)} %get-tuple-element.31), channel_id=1, source_target_pairs={{1,0},{2,1},{3,2},{5,4},{6,5},{7,6},{9,8},{10,9},{11,10},{13,12},{... | collective-permute-start | bytes 393224 | tf_op jit(solution)/shard_map/ppermute | solution.py:15
  19.0 5.4 %collective-permute-start.2 = (bf16[4,10,32,512]{3,2,1,0:T(8,128)(2,1)S(1)}, bf16[4,10,32,512]{3,2,1,0:T(8,128)(2,1)S(1)}, u32[]{:S(2)}, u32[]{:S(2)}) collective-permute-start(bf16[4,10,32,512]{3,2,1,0:T(8,128)(2,1)S(1)} %constant_dynamic-update-slice_fusion), channel_id=1, source_target_pairs={{0,4},{4,0},{1,5},{5,1},{2,6},{6,2},{3,7},{7,3},{8,12},{12,8},{9,1... | collective-permute-start | bytes 3932168 | tf_op jit(solution)/shard_map/ppermute | solution.py:19
  107.2 11.7 %copy-start.16 = (f32[64]{0:T(128)S(1)}, f32[64]{0:T(128)}, u32[]{:S(2)}) copy-start(f32[64]{0:T(128)} %get-tuple-element.50) | copy-start | bytes 772
  107.2 11.7 %copy-start.17 = (f32[64]{0:T(128)S(1)}, f32[64]{0:T(128)}, u32[]{:S(2)}) copy-start(f32[64]{0:T(128)} %get-tuple-element.51) | copy-start | bytes 772
  107.2 11.7 %copy-start.18 = (f32[64]{0:T(128)S(1)}, f32[64]{0:T(128)}, u32[]{:S(2)}) copy-start(f32[64]{0:T(128)} %get-tuple-element.52) | copy-start | bytes 772
  107.3 11.7 %copy-start.19 = (f32[64]{0:T(128)S(1)}, f32[64]{0:T(128)}, u32[]{:S(2)}) copy-start(f32[64]{0:T(128)} %get-tuple-element.53) | copy-start | bytes 772
  107.3 11.7 %copy-start.20 = (f32[64]{0:T(128)S(1)}, f32[64]{0:T(128)}, u32[]{:S(2)}) copy-start(f32[64]{0:T(128)} %get-tuple-element.54) | copy-start | bytes 772
  107.3 11.7 %copy-start.21 = (f32[64]{0:T(128)S(1)}, f32[64]{0:T(128)}, u32[]{:S(2)}) copy-start(f32[64]{0:T(128)} %get-tuple-element.55) | copy-start | bytes 772
  107.3 11.7 %copy-start.22 = (f32[64]{0:T(128)S(1)}, f32[64]{0:T(128)}, u32[]{:S(2)}) copy-start(f32[64]{0:T(128)} %get-tuple-element.65) | copy-start | bytes 772
  107.3 11.7 %copy-start.23 = (f32[64]{0:T(128)S(1)}, f32[64]{0:T(128)}, u32[]{:S(2)}) copy-start(f32[64]{0:T(128)} %get-tuple-element.66) | copy-start | bytes 772
  107.3 11.7 %copy-start.24 = (f32[64]{0:T(128)S(1)}, f32[64]{0:T(128)}, u32[]{:S(2)}) copy-start(f32[64]{0:T(128)} %get-tuple-element.67) | copy-start | bytes 772
  107.3 11.7 %copy-start.25 = (f32[64]{0:T(128)S(1)}, f32[64]{0:T(128)}, u32[]{:S(2)}) copy-start(f32[64]{0:T(128)} %get-tuple-element.68) | copy-start | bytes 772
  107.3 11.7 %copy-start.26 = (f32[64]{0:T(128)S(1)}, f32[64]{0:T(128)}, u32[]{:S(2)}) copy-start(f32[64]{0:T(128)} %get-tuple-element.69) | copy-start | bytes 772
  107.3 11.7 %copy-start.27 = (f32[64]{0:T(128)S(1)}, f32[64]{0:T(128)}, u32[]{:S(2)}) copy-start(f32[64]{0:T(128)} %get-tuple-element.70) | copy-start | bytes 772
  107.3 11.7 %copy-start.28 = (f32[64]{0:T(128)S(1)}, f32[64]{0:T(128)}, u32[]{:S(2)}) copy-start(f32[64]{0:T(128)} %get-tuple-element.71) | copy-start | bytes 772
  113.2 6.1 %collective-permute-start.5 = (bf16[8,32,512]{2,1,0:T(8,128)(2,1)}, bf16[8,32,512]{2,1,0:T(8,128)(2,1)S(1)}, u32[]{:S(2)}, u32[]{:S(2)}) collective-permute-start(bf16[8,32,512]{2,1,0:T(8,128)(2,1)} %shard_map.74), channel_id=1, source_target_pairs={{0,24},{1,25},{2,26},{3,27},{4,28},{5,29},{6,30},{7,31}} | collective-permute-start | bytes 786440 | tf_op jit(solution)/shard_map/ppermute | solution.py:15
  113.9 15.4 %collective-permute-start.4 = (bf16[8,32,512]{2,1,0:T(8,128)(2,1)}, bf16[8,32,512]{2,1,0:T(8,128)(2,1)S(1)}, u32[]{:S(2)}, u32[]{:S(2)}) collective-permute-start(bf16[8,32,512]{2,1,0:T(8,128)(2,1)} %shard_map.74), channel_id=1, source_target_pairs={{0,16},{8,24},{1,17},{9,25},{2,18},{10,26},{3,19},{11,27},{4,20},{... | collective-permute-start | bytes 786440 | tf_op jit(solution)/shard_map/ppermute | solution.py:15
  115.2 14.2 %collective-permute-start.3 = (bf16[8,32,512]{2,1,0:T(8,128)(2,1)}, bf16[8,32,512]{2,1,0:T(8,128)(2,1)S(1)}, u32[]{:S(2)}, u32[]{:S(2)}) collective-permute-start(bf16[8,32,512]{2,1,0:T(8,128)(2,1)} %shard_map.74), channel_id=1, source_target_pairs={{0,8},{8,16},{16,24},{1,9},{9,17},{17,25},{2,10},{10,18},{18,26},{... | collective-permute-start | bytes 786440 | tf_op jit(solution)/shard_map/ppermute | solution.py:15
  119.3 10.4 %copy-start.3 = (f32[8,32,512]{2,1,0:T(8,128)S(1)}, f32[8,32,512]{2,1,0:T(8,128)}, u32[]{:S(2)}) copy-start(f32[8,32,512]{2,1,0:T(8,128)} %maximum_select_fusion.1.begin_ref) | copy-start | bytes 1572868
  137.9 7.1 %collective-permute-start.7 = (bf16[8,1,32,512]{3,2,1,0:T(8,128)(2,1)S(1)}, bf16[8,1,32,512]{3,2,1,0:T(8,128)(2,1)S(1)}, u32[]{:S(2)}, u32[]{:S(2)}) collective-permute-start(bf16[8,1,32,512]{3,2,1,0:T(8,128)(2,1)S(1)} %get-tuple-element.20), channel_id=1, source_target_pairs={{1,0},{2,1},{3,2},{5,4},{6,5},{7,6},{9,8},{10,9},{11,10},{13,12},{... | collective-permute-start | bytes 786440 | tf_op jit(solution)/shard_map/ppermute | solution.py:15
  139.2 7.3 %collective-permute-start.6 = (bf16[8,1,32,512]{3,2,1,0:T(8,128)(2,1)S(1)}, bf16[8,1,32,512]{3,2,1,0:T(8,128)(2,1)S(1)}, u32[]{:S(2)}, u32[]{:S(2)}) collective-permute-start(bf16[8,1,32,512]{3,2,1,0:T(8,128)(2,1)S(1)} %get-tuple-element.19), channel_id=1, source_target_pairs={{0,1},{1,2},{2,3},{4,5},{5,6},{6,7},{8,9},{9,10},{10,11},{12,13},{... | collective-permute-start | bytes 786440 | tf_op jit(solution)/shard_map/ppermute | solution.py:15
  158.7 14.6 %collective-permute-start.8 = (bf16[4,8,32,512]{3,1,2,0:T(8,128)(2,1)S(1)}, bf16[4,8,32,512]{3,1,2,0:T(8,128)(2,1)S(1)}, u32[]{:S(2)}, u32[]{:S(2)}) collective-permute-start(bf16[4,8,32,512]{3,1,2,0:T(8,128)(2,1)S(1)} %slice_bitcast_fusion.1), channel_id=1, source_target_pairs={{0,4},{4,0},{1,5},{5,1},{2,6},{6,2},{3,7},{7,3},{8,12},{12,8},{9,1... | collective-permute-start | bytes 3145736 | tf_op jit(solution)/shard_map/ppermute | solution.py:19
  (17 other events, 67.2 us)
where the time goes:
time: 181 us; the launch traced here: 180 us
  Pallas kernels  93.2 us (51%)
  local copies, waits for them, and re-layouts  23.8 us (13%)
  starting transfers between devices  20.8 us (11%)
  other arithmetic  15.6 us (9%)
  waiting for transfers between devices  13.2 us (7%)
  matrix products  12.6 us (7%)
    pallas_call x1, Pallas kernels, drive(): pl.pallas_call(functools.partial(drive_kernel, chips, rows), out_shape=(j...  80.9 us
    ppermute x7, starting transfers between devices, shifted(): return lax.ppermute(value, axis, pairs)  16.1 us
    ppermute x7, waiting for transfers between devices, shifted(): return lax.ppermute(value, axis, pairs)  13.2 us
    conv_general_dilated x2, matrix products, conv(): lax.conv_general_dilated(field, weight, (1, 1), ((0, 0), (1, 1)), dimensi...  12.6 us
    pallas_call x2, Pallas kernels, recur(): pl.pallas_call(functools.partial(recur_kernel, last_only), out_shape=jax....  12.2 us
    unnamed x76, local copies, waits for them, and re-layouts  8.97 us
    convert_element_type x1, other arithmetic, on_device(): return jax.nn.gelu(pre_act, approximate=False).astype(jnp.bfloat16)  5.2 us
    ppermute x2, starting transfers between devices, swapped(): return lax.ppermute(value, CORE, [(0, 1), (1, 0)])  4.64 us
  transfers between devices with their start and end apart: 9, of which 3 were waited for; matrix products, arithmetic and copies ran while one was open for 15% of the time, Pallas kernels for 0%

commit v1 on v0

--- a/solution.py
+++ b/solution.py
@@ -366,7 +366,696 @@
     return modulus * jnp.cos(angle * exponent), modulus * jnp.sin(angle * exponent)
 
 
+ORDER = (1, 0, 2)
+
+
+def power(re, im, exponent):
+    out_re, out_im = jnp.ones_like(re), jnp.zeros_like(im)
+    while exponent:
+        if exponent % 2:
+            out_re, out_im = out_re * re - out_im * im, out_re * im + out_im * re
+        re, im = re * re - im * im, 2.0 * (re * im)
+        exponent //= 2
+    return out_re, out_im
+
+
+def layer_kernel(
+    win, wout, frames, begin, rate, angle, skip, out,
+    views, full_in, full_out, driven, held, acc, tail, tail_half, met, joint, far_joint, given, got,
+    z_send, z_recv, x_send, x_recv, y_send, y_recv,
+    halo_send, halo_recv, pass_send, pass_recv, edge_send, edge_recv,
+    first_send, first_recv, second_send, second_recv, swap_send, swap_recv, part_send, part_recv, local,
+):
+    chip, core, row = (lax.axis_index(a) for a in (CHIPS, CORE, ROWS))
+    rows = lax.axis_size(ROWS)
+    other = 1 - core
+    beside = chip + 1 - 2 * (chip % 2)
+    across = (chip + 2) % 4
+    opposite = 3 - chip
+    _, many, padded, columns, channels = views.shape
+    band, mine = padded - 2, many // 2
+    lanes = tail.shape[-1] // 2
+    depth = 3 * channels
+    own = row // 2 == core
+    near = jnp.where(row <= 2 * core, 0, 1)
+    slots = (near, 1 - near)
+    here = pl.multiple_of(core * mine, mine)
+    there = pl.multiple_of(other * mine, mine)
+    has_up, has_down = row > 0, row < rows - 1
+
+    def remote(src, dst, send, recv, **where):
+        return pltpu.make_async_remote_copy(
+            src_ref=src, dst_ref=dst, send_sem=send, recv_sem=recv,
+            device_id=where, device_id_type=pl.DeviceIdType.MESH,
+        )
+
+    def block(w, slot, quarter, o):
+        a = ORDER[o]
+        if w == 0:
+            return full_in.at[slot, :, quarter, :, a * depth : (a + 1) * depth]
+        return full_out.at[a, :, slot, :, quarter]
+
+    def source(w, quarter, o):
+        a = ORDER[o]
+        if w == 0:
+            return win.at[:, quarter, :, a * depth : (a + 1) * depth]
+        return wout.at[a, :, :, quarter]
+
+    def z_piece(k):
+        return (chip, k) if k < 3 else (opposite, 2)
+
+    def z_copy(w, slot, k, kind, first, to):
+        quarter, o = z_piece(k)
+        dst = block(w, slot, quarter, o)
+        src = source(w, quarter, o) if first else dst
+        return remote(src, dst, z_send.at[w, kind, k], z_recv.at[w, slot, k], **{ROWS: to})
+
+    def x_copy(w, rank, i):
+        quarter, o = (chip, i) if i < 3 else (across, 1)
+        ref = block(w, slots[rank], quarter, o)
+        return remote(ref, ref, x_send.at[w, rank, i], x_recv.at[w, rank, i], **{CHIPS: beside})
+
+    def y_copy(w, rank, i):
+        quarter, o = (chip, i) if i < 3 else (beside, 0)
+        ref = block(w, slots[rank], quarter, o)
+        return remote(ref, ref, y_send.at[w, rank, i], y_recv.at[w, rank, i], **{CHIPS: across})
+
+    def x_came(w, rank, i):
+        quarter, o = (beside, i) if i < 3 else (opposite, 1)
+        ref = block(w, slots[rank], quarter, o)
+        remote(ref, ref, x_send.at[w, rank, i], x_recv.at[w, rank, i], **{CHIPS: beside}).wait_recv()
+
+    def y_came(w, rank, i):
+        quarter, o = (across, i) if i < 3 else (opposite, 0)
+        ref = block(w, slots[rank], quarter, o)
+        remote(ref, ref, y_send.at[w, rank, i], y_recv.at[w, rank, i], **{CHIPS: across}).wait_recv()
+
+    def apart(rank):
+        return jnp.logical_not(own) if rank == 0 else jnp.logical_or(own, True)
+
+    def from_below(rank):
+        return 2 * core + slots[rank] > row
+
+    def relays(rank):
+        below = from_below(rank)
+        return (
+            jnp.logical_and(apart(rank), jnp.logical_and(below, has_up)),
+            jnp.logical_and(apart(rank), jnp.logical_and(jnp.logical_not(below), has_down)),
+        )
+
+    def guarded(rank, do):
+        if rank == 0:
+            pl.when(apart(0))(do)
+        else:
+            do()
+
+    def send_own(w):
+        for k in range(4):
+            @pl.when(jnp.logical_and(own, has_up))
+            def _():
+                z_copy(w, near, k, 0, True, row - 1).start()
+
+            @pl.when(jnp.logical_and(own, has_down))
+            def _():
+                z_copy(w, near, k, 2, True, row + 1).start()
+
+    def z_event(w, rank, k):
+        slot = slots[rank]
+
+        def do():
+            z_copy(w, slot, k, rank, False, row).wait_recv()
+            if k < 3:
+                x_copy(w, rank, k).start()
+                y_copy(w, rank, k).start()
+
+        guarded(rank, do)
+        up, down = relays(rank)
+
+        @pl.when(up)
+        def _():
+            z_copy(w, slot, k, rank, False, row - 1).start()
+
+        @pl.when(down)
+        def _():
+            z_copy(w, slot, k, rank, False, row + 1).start()
+
+    def x_event(w, rank):
+        def do():
+            x_came(w, rank, 0)
+            y_copy(w, rank, 3).start()
+
+        guarded(rank, do)
+
+    def y_event(w, rank):
+        def do():
+            y_came(w, rank, 1)
+            x_copy(w, rank, 3).start()
+
+        guarded(rank, do)
+
+    def events(w, rank):
+        return [
+            functools.partial(z_event, w, rank, 0),
+            functools.partial(z_event, w, rank, 1),
+            functools.partial(x_event, w, rank),
+            functools.partial(z_event, w, rank, 2),
+            functools.partial(y_event, w, rank),
+            functools.partial(z_event, w, rank, 3),
+        ]
+
+    def complete(w, rank, o):
+        def do():
+            if o != 0:
+                x_came(w, rank, o)
+            else:
+                y_came(w, rank, 3)
+            if o != 1:
+                y_came(w, rank, o)
+            else:
+                x_came(w, rank, 3)
+
+        guarded(rank, do)
+
+    def settle(w):
+        for k in range(4):
+            @pl.when(jnp.logical_and(own, has_up))
+            def _():
+                z_copy(w, near, k, 0, True, row - 1).wait_send()
+
+            @pl.when(jnp.logical_and(own, has_down))
+            def _():
+                z_copy(w, near, k, 2, True, row + 1).wait_send()
+
+            for rank in range(2):
+                up, down = relays(rank)
+
+                @pl.when(jnp.logical_or(up, down))
+                def _():
+                    z_copy(w, slots[rank], k, rank, False, row).wait_send()
+
+        for rank in range(2):
+            def do():
+                for i in range(4):
+                    x_copy(w, rank, i).wait_send()
+                    y_copy(w, rank, i).wait_send()
+
+            guarded(rank, do)
+
+    barrier = pltpu.get_barrier_semaphore()
+
+    def greet(**where):
+        pl.semaphore_signal(barrier, inc=1, device_id=where, device_id_type=pl.DeviceIdType.MESH)
+
+    greet(**{CORE: other})
+    greet(**{CHIPS: beside})
+    greet(**{CHIPS: across})
+
+    @pl.when(has_up)
+    def _():
+        greet(**{ROWS: row - 1})
+
+    @pl.when(has_down)
+    def _():
+        greet(**{ROWS: row + 1})
+
+    pl.semaphore_wait(barrier, 3 + (row + rows - 1) // rows + (2 * rows - 2 - row) // rows)
+
+    mine_in = views.at[1, pl.ds(here, mine), 1 : band + 1]
+    keep = pltpu.make_async_copy(frames, mine_in, local.at[0])
+    hold_in = pltpu.make_async_copy(win, full_in.at[near], local.at[1])
+    hold_out = pltpu.make_async_copy(wout, full_out.at[:, :, near], local.at[2])
+    swap = remote(frames, mine_in, swap_send, swap_recv, **{CORE: other})
+    theirs_in = views.at[1, pl.ds(there, mine), 1 : band + 1]
+
+    def halo(side, start):
+        at = views.at[1, pl.ds(here, mine), band + 1 if side == 0 else 0]
+        src = frames.at[:, 0 if side == 0 else band - 1]
+        return remote(src, at, halo_send.at[side], halo_recv.at[side], **{ROWS: row - 1 if side == 0 else row + 1})
+
+    def halo_at(side, first):
+        return views.at[1, pl.ds(first, mine), band + 1 if side == 0 else 0]
+
+    def halo_came(side):
+        ref = halo_at(side, here)
+        remote(ref, ref, halo_send.at[side], halo_recv.at[side], **{ROWS: row}).wait_recv()
+
+    def handed(side, first):
+        ref = halo_at(side, first)
+        return remote(ref, ref, pass_send.at[side], pass_recv.at[side], **{CORE: other})
+
+    gives = (has_up, has_down)
+    takes = (has_down, has_up)
+
+    swap.start()
+    keep.start()
+    for side in range(2):
+        @pl.when(gives[side])
+        def _():
+            halo(side, True).start()
+
+    send_own(0)
+
+    @pl.when(own)
+    def _():
+        hold_in.start()
+        hold_out.start()
+
+    blank = jnp.zeros((columns, channels), views.dtype)
+    for side in range(2):
+        edge = band + 1 if side == 0 else 0
+
+        @pl.when(jnp.logical_not(takes[side]))
+        def _():
+            @pl.loop(0, many)
+            def _(f):
+                views[1, f, edge] = blank
+                for slot in range(2):
+                    held[slot, 1, f, edge] = blank[:, : 2 * lanes]
+
+    place = lax.broadcasted_iota(jnp.int32, (columns, 1), 0)
+    not_first, not_last = place > 0, place < columns - 1
+
+    def sides(wide):
+        before = jnp.where(not_first, pltpu.roll(wide, 1, 0), 0.0)
+        after = jnp.where(not_last, pltpu.roll(wide, columns - 1, 0), 0.0)
+        return before.astype(views.dtype), after.astype(views.dtype)
+
+    def spread_views(first, count):
+        @pl.loop(0, count)
+        def _(i):
+            f = first + i
+
+            @pl.loop(0, padded)
+            def _(r):
+                views[0, f, r], views[2, f, r] = sides(views[1, f, r].astype(jnp.float32))
+
+    def drive(rank, o, m0, m1):
+        slot, a = slots[rank], ORDER[o]
+
+        @pl.loop(m0, m1)
+        def _(m):
+            at = pl.ds(m * 2, 2)
+            pixels = 2 * band * columns
+            window = jnp.concatenate(
+                [views[b, at, a : a + band].reshape(pixels, channels) for b in range(3)], axis=1
+            )
+            weight = full_in[slot, :, :, :, a * depth : (a + 1) * depth].reshape(2 * lanes, depth)
+            result = lax.dot_general(
+                window, weight, (((1,), (1,)), ((), ())), preferred_element_type=jnp.float32
+            ).reshape(2, band, columns, 2 * lanes)
+            if o == 0:
+                driven[slot, at] = result
+            else:
+                driven[slot, at] += result
+
+    blocks = many // 2
+
+    def factors(rank):
+        at = pl.ds(2 * core + slots[rank], 1)
+        modulus = jnp.exp(-rate[at, :])
+        return modulus * jnp.cos(angle[at, :]), modulus * jnp.sin(angle[at, :])
+
+    def ends(rank):
+        slot = slots[rank]
+        lam_re, lam_im = factors(rank)
+
+        @pl.loop(0, band)
+        def _(r):
+            re, im = begin[slot, r, :, :lanes], begin[slot, r, :, lanes:]
+            for t in range(many):
+                re, im = (
+                    lam_re * re - lam_im * im + driven[slot, t, r, :, :lanes],
+                    lam_re * im + lam_im * re + driven[slot, t, r, :, lanes:],
+                )
+            tail[slot, r, :, :lanes] = re
+            tail[slot, r, :, lanes:] = im
+            tail_half[slot, r, :, :lanes] = re.astype(tail_half.dtype)
+            tail_half[slot, r, :, lanes:] = im.astype(tail_half.dtype)
+
+    tells, hears = chip < 3, chip != 2
+    joins = chip < 2
+
+    def first_copy(rank):
+        slot = slots[rank]
+        return remote(
+            tail_half.at[slot], met.at[slot], first_send.at[rank], first_recv.at[rank], **{CHIPS: beside}
+        )
+
+    def second_copy(rank):
+        slot = slots[rank]
+        return remote(
+            joint.at[slot], far_joint.at[slot], second_send.at[rank], second_recv.at[rank], **{CHIPS: across}
+        )
+
+    def tell(rank):
+        @pl.when(tells)
+        def _():
+            first_copy(rank).start()
+
+    def merge(rank):
+        slot = slots[rank]
+        lam_re, lam_im = factors(rank)
+        jump_re, jump_im = power(lam_re, lam_im, many)
+
+        def combine(r, late_re, late_im, early_re, early_im):
+            return (
+                late_re + jump_re * early_re - jump_im * early_im,
+                late_im + jump_re * early_im + jump_im * early_re,
+            )
+
+        def split(ref, r):
+            return ref[slot, r, :, :lanes].astype(jnp.float32), ref[slot, r, :, lanes:].astype(jnp.float32)
+
+        def put(ref, r, value):
+            ref[slot, r, :, :lanes] = value[0].astype(ref.dtype)
+            ref[slot, r, :, lanes:] = value[1].astype(ref.dtype)
+
+        @pl.when(hears)
+        def _():
+            first_copy(rank).wait_recv()
+
+        @pl.when(chip == 0)
+        def _():
+            @pl.loop(0, band)
+            def _(r):
+                put(joint, r, combine(r, *split(met, r), *split(tail, r)))
+                put(tail, r, split(begin, r))
+
+        @pl.when(chip == 1)
+        def _():
+            @pl.loop(0, band)
+            def _(r):
+                put(joint, r, combine(r, *split(tail, r), *split(met, r)))
+                put(tail, r, split(met, r))
+
+        @pl.when(joins)
+        def _():
+            second_copy(rank).start()
+
+    def carry(rank):
+        slot = slots[rank]
+        lam_re, lam_im = factors(rank)
+        jump_re, jump_im = power(lam_re, lam_im, many)
+
+        @pl.when(jnp.logical_not(joins))
+        def _():
+            second_copy(rank).wait_recv()
+
+        @pl.when(chip == 2)
+        def _():
+            @pl.loop(0, band)
+            def _(r):
+                tail[slot, r] = far_joint[slot, r].astype(jnp.float32)
+
+        @pl.when(chip == 3)
+        def _():
+            @pl.loop(0, band)
+            def _(r):
+                late, early = met[slot, r].astype(jnp.float32), far_joint[slot, r].astype(jnp.float32)
+                re, im = early[:, :lanes], early[:, lanes:]
+                tail[slot, r, :, :lanes] = late[:, :lanes] + jump_re * re - jump_im * im
+                tail[slot, r, :, lanes:] = late[:, lanes:] + jump_re * im + jump_im * re
+
+    def scan_rows(rank, start, count, stride):
+        slot = slots[rank]
+        lam_re, lam_im = factors(rank)
+
+        @pl.loop(0, count)
+        def _(i):
+            r = start + i * stride
+            re, im = tail[slot, r, :, :lanes], tail[slot, r, :, lanes:]
+            for t in range(many):
+                re, im = (
+                    lam_re * re - lam_im * im + driven[slot, t, r, :, :lanes],
+                    lam_re * im + lam_im * re + driven[slot, t, r, :, lanes:],
+                )
+                for part, value in enumerate((re, im)):
+                    at = slice(part * lanes, (part + 1) * lanes)
+                    before, after = sides(value)
+                    held[slot, 0, t, 1 + r, :, at] = before
+                    held[slot, 1, t, 1 + r, :, at] = value.astype(held.dtype)
+                    held[slot, 2, t, 1 + r, :, at] = after
+
+    def edge_copy(rank, side):
+        slot = slots[rank]
+        return remote(
+            held.at[slot, 1, :, 1 if side == 0 else band],
+            held.at[slot, 1, :, band + 1 if side == 0 else 0],
+            edge_send.at[rank, side],
+            edge_recv.at[slot, side],
+            **{ROWS: row - 1 if side == 0 else row + 1},
+        )
+
+    def scan(rank):
+        scan_rows(rank, 0, 2, band - 1)
+        scan_rows(rank, 1, (band - 2) // 2, 1)
+        for side in range(2):
+            @pl.when(gives[side])
+            def _():
+                edge_copy(rank, side).start()
+        scan_rows(rank, 1 + (band - 2) // 2, band - 2 - (band - 2) // 2, 1)
+
+    def edges_came(rank):
+        slot = slots[rank]
+        for side in range(2):
+            at = band + 1 if side == 0 else 0
+            ref = held.at[slot, 1, :, at]
+
+            @pl.when(takes[side])
+            def _():
+                remote(
+                    ref, ref, edge_send.at[rank, side], edge_recv.at[slot, side], **{ROWS: row}
+                ).wait_recv()
+
+            @pl.loop(0, many)
+            def _(f):
+                held[slot, 0, f, at], held[slot, 2, f, at] = sides(held[slot, 1, f, at].astype(jnp.float32))
+
+    def mix_block(rank, rights, first, fresh):
+        slot = slots[rank]
+        pixels = 2 * band * columns
+        window = jnp.concatenate(
+            [
+                held[slot, b, pl.ds(first, 2), a : a + band].reshape(pixels, 2 * lanes)
+                for a in rights
+                for b in range(3)
+            ],
+            axis=1,
+        )
+        weight = jnp.concatenate([full_out[a, :, slot].reshape(6 * lanes, channels) for a in rights], axis=0)
+        result = jnp.dot(window, weight, preferred_element_type=jnp.float32)
+        result = result.reshape(2, band, columns, channels)
+        if fresh:
+            return result
+        return acc[pl.ds(first, 2)] + result
+
+    def mix(rank, rights, fresh):
+        @pl.loop(0, blocks)
+        def _(m):
+            acc[pl.ds(m * 2, 2)] = mix_block(rank, rights, m * 2, fresh)
+
+    def part_copy(m):
+        at = pl.ds(m * 2, 2)
+        return remote(
+            given.at[at], got.at[at], part_send.at[m], part_recv.at[m], **{CORE: other}
+        )
+
+    def mix_last(rank, rights):
+        for m in range(blocks // 2):
+            given[m * 2 : m * 2 + 2] = mix_block(rank, rights, there + m * 2, False).astype(given.dtype)
+            part_copy(m).start()
+        for m in range(blocks // 2):
+            acc[pl.ds(here + m * 2, 2)] = mix_block(rank, rights, here + m * 2, False)
+        for m in range(blocks // 2):
+            part_copy(m).wait_recv()
+
+            @pl.loop(0, 2)
+            def _(i):
+                f = m * 2 + i
+
+                @pl.loop(0, band)
+                def _(r):
+                    value = acc[here + f, r] + got[f, r].astype(jnp.float32)
+                    value = value + skip[...] * views[1, here + f, 1 + r].astype(jnp.float32)
+                    out[f, r] = (0.5 * value * (1.0 + lax.erf(value * 0.7071067811865476))).astype(out.dtype)
+
+    steps = iter(events(0, 0))
+    next(steps)()
+    keep.wait()
+    for side in range(2):
+        @pl.when(takes[side])
+        def _():
+            halo_came(side)
+            handed(side, here).start()
+
+    next(steps)()
+    spread_views(here, mine // 2)
+    next(steps)()
+    spread_views(here + mine // 2, mine // 2)
+    next(steps)()
+    remote(theirs_in, theirs_in, swap_send, swap_recv, **{CORE: other}).wait_recv()
+    for side in range(2):
+        @pl.when(takes[side])
+        def _():
+            handed(side, there).wait_recv()
+
+    spread_views(there, mine // 2)
+    next(steps)()
+    spread_views(there + mine // 2, mine // 2)
+    next(steps)()
+
+    @pl.when(own)
+    def _():
+        hold_in.wait()
+        hold_out.wait()
+
+    steps = iter(events(0, 1))
+    for o in range(3):
+        next(steps)()
+        complete(0, 0, o)
+        drive(0, o, 0, blocks // 2)
+        next(steps)()
+        drive(0, o, blocks // 2, blocks)
+    send_own(1)
+    ends(0)
+    tell(0)
+    steps = iter(events(1, 0))
+    complete(0, 1, 0)
+    drive(1, 0, 0, blocks)
+    next(steps)()
+    complete(0, 1, 1)
+    merge(0)
+    drive(1, 1, 0, blocks)
+    next(steps)()
+    complete(0, 1, 2)
+    drive(1, 2, 0, blocks)
+    ends(1)
+    tell(1)
+    for step in steps:
+        step()
+    carry(0)
+    scan(0)
+    merge(1)
+    steps = iter(events(1, 1))
+    next(steps)()
+    next(steps)()
+    complete(1, 0, 0)
+    mix(0, (1,), True)
+    carry(1)
+    scan(1)
+    for step in steps:
+        step()
+    edges_came(0)
+    complete(1, 0, 1)
+    complete(1, 0, 2)
+    mix(0, (0, 2), False)
+    complete(1, 1, 0)
+    mix(1, (1,), False)
+    edges_came(1)
+    complete(1, 1, 1)
+    complete(1, 1, 2)
+    mix_last(1, (0, 2))
+
+    settle(0)
+    settle(1)
+    swap.wait_send()
+    for side in range(2):
+        @pl.when(gives[side])
+        def _():
+            halo(side, False).wait_send()
+            for rank in range(2):
+                edge_copy(rank, side).wait_send()
+
+        @pl.when(takes[side])
+        def _():
+            handed(side, here).wait_send()
+
+    for rank in range(2):
+        @pl.when(tells)
+        def _():
+            first_copy(rank).wait_send()
+
+        @pl.when(joins)
+        def _():
+            second_copy(rank).wait_send()
+
+    for m in range(blocks // 2):
+        part_copy(m).wait_send()
+
+
+def layer(weight_in, weight_out, frames_in, start, log_decay, rotation, skip_gain):
+    count, band, columns, channels = frames_in.shape
+    lanes = weight_in.shape[1]
+    quarter = lanes // 4
+    many = 2 * count
+    vmem, anywhere = pl.BlockSpec(memory_space=pltpu.VMEM), pl.BlockSpec(memory_space=pl.ANY)
+    dma = pltpu.SemaphoreType.DMA
+    half = frames_in.dtype
+    full = jnp.float32
+    return pl.pallas_call(
+        layer_kernel,
+        out_shape=jax.ShapeDtypeStruct(frames_in.shape, half),
+        in_specs=[anywhere, anywhere, anywhere, vmem, vmem, vmem, vmem],
+        out_specs=vmem,
+        scratch_shapes=[
+            pltpu.VMEM((3, many, band + 2, columns, channels), half),
+            pltpu.VMEM((2, 2, 4, quarter, 9 * channels), half),
+            pltpu.VMEM((3, 3, 2, 2, 4, quarter, channels), half),
+            pltpu.VMEM((2, many, band, columns, 2 * lanes), full),
+            pltpu.VMEM((2, 3, many, band + 2, columns, 2 * lanes), half),
+            pltpu.VMEM((many, band, columns, channels), full),
+            pltpu.VMEM((2, band, columns, 2 * lanes), full),
+            pltpu.VMEM((2, band, columns, 2 * lanes), half),
+            pltpu.VMEM((2, band, columns, 2 * lanes), half),
+            pltpu.VMEM((2, band, columns, 2 * lanes), half),
+            pltpu.VMEM((2, band, columns, 2 * lanes), half),
+            pltpu.VMEM((count, band, columns, channels), half),
+            pltpu.VMEM((count, band, columns, channels), half),
+            dma((2, 3, 4)), dma((2, 2, 4)), dma((2, 2, 4)), dma((2, 2, 4)), dma((2, 2, 4)), dma((2, 2, 4)),
+            dma((2,)), dma((2,)), dma((2,)), dma((2,)), dma((2, 2)), dma((2, 2)),
+            dma((2,)), dma((2,)), dma((2,)), dma((2,)), dma, dma,
+            dma((many // 4,)), dma((many // 4,)), dma((3,)),
+        ],
+        compiler_params=pltpu.CompilerParams(
+            collective_id=3, has_side_effects=True, vmem_limit_bytes=63 * 1024 * 1024
+        ),
+    )(
+        weight_in.reshape(2, 4, quarter, 9 * channels),
+        weight_out.reshape(3, 3, 2, 4, quarter, channels),
+        frames_in,
+        start,
+        log_decay.reshape(-1, lanes),
+        rotation.reshape(-1, lanes),
+        skip_gain.reshape(1, channels),
+    )
+
+
+def fused(frames_in, weight_in, weight_out, log_decay, rotation, start_state, skip_gain):
+    core, chip = lax.axis_index(CORE), lax.axis_index(CHIPS)
+    lanes = weight_in.shape[1]
+    band, columns = start_state.shape[:2]
+    start = lax.dynamic_slice_in_dim(start_state, core * 2 * lanes, 2 * lanes, 3)
+    start = start.reshape(band, columns, 2, 2, lanes).transpose(3, 0, 1, 2, 4)
+    start = jnp.where(chip == 0, start, jnp.float32(0.0)).reshape(2, band, columns, 2 * lanes)
+    return layer(weight_in, weight_out, frames_in, start, log_decay, rotation, skip_gain)
+
+
+def fits(frames_in, weight_in):
+    count, band, columns, channels = frames_in.shape
+    chips, cores, rows = (lax.axis_size(a) for a in (CHIPS, CORE, ROWS))
+    return (
+        (chips, rows) == (4, 2 * cores)
+        and weight_in.shape[1] % 128 == 0
+        and channels % 128 == 0
+        and columns % 16 == 0
+        and band >= 4
+        and count % 4 == 0
+    )
+
+
 def on_device(frames_in, weight_in, weight_out, log_decay, rotation, start_state, skip_gain):
+    if fits(frames_in, weight_in):
+        return fused(frames_in, weight_in, weight_out, log_decay, rotation, start_state, skip_gain)
     frame_count, band_rows, columns, channels = frames_in.shape
     shard = weight_in.shape[1]
     chips, cores, rows = (lax.axis_size(a) for a in (CHIPS, CORE, ROWS))

time: 181 us -> 92.8 us (0.51)
  starting transfers between devices: 20.8 us -> 0 us
  local copies, waits for them, and re-layouts: 23.8 us -> 3.52 us
  other arithmetic: 15.6 us -> 1.31 us
  waiting for transfers between devices: 13.2 us -> 0 us
  matrix products: 12.6 us -> 0 us
  Pallas kernels: 93.2 us -> 87.7 us
    ppermute x9 -> x0, starting transfers between devices: 20.8 us -> none  [the longest x7 16.1 us: shifted(): return lax.ppermute(value, axis, pairs)]
    ppermute x9 -> x0, waiting for transfers between devices: 13.2 us -> none  [the longest x7 13.2 us: shifted(): return lax.ppermute(value, axis, pairs)]
    conv_general_dilated x2 -> x0, matrix products: 12.6 us -> none  [conv(): lax.conv_general_dilated(field, weight, (1, 1), ((0, 0), (1, 1)), dimensi...]
    slice x5 -> x0, local copies, waits for them, and re-layouts: 6.97 us -> none  [the longest x3 4.06 us: own(): lax.slice_in_dim(vector, r * shard + c * half, r * shard + (c + 1) * half...]
    unnamed x76 -> x1, local copies, waits for them, and re-layouts: 8.97 us -> 2.3 us
    pallas_call x3 -> x1, Pallas kernels: 93.2 us -> 87.7 us  [layer(): pl.pallas_call(layer_kernel, out_shape=jax.ShapeDtypeStruct(frames_in.sha...]
    convert_element_type x4 -> x0, other arithmetic: 5.35 us -> none  [the longest x1 5.2 us: on_device(): return jax.nn.gelu(pre_act, approximate=False).astype(jnp.bfloat16)]
    dynamic_slice x5 -> x0, local copies, waits for them, and re-layouts: 3.79 us -> none  [the longest x1 1.17 us: on_device(): slice_in = lax.dynamic_slice_in_dim(weight_in, core * half, half, 1)]
  transfers between devices with their start and end apart: 9 -> 0, of which waited for: 3 -> 0; matrix products, arithmetic and copies ran while one was open for 15% -> 0% of each run, Pallas kernels for 0% -> 0%
where the time goes in v1:
time: 92.8 us; the launch traced here: 92.6 us
  Pallas kernels  87.7 us (95%)
  local copies, waits for them, and re-layouts  3.52 us (4%)
  other arithmetic  1.31 us (1%)
    pallas_call x1, Pallas kernels, layer(): pl.pallas_call(layer_kernel, out_shape=jax.ShapeDtypeStruct(frames_in.sha...  87.7 us
    unnamed x1, local copies, waits for them, and re-layouts  2.3 us

profile of v1, /device:TPU:5, one launch (start us, length us, event | category | flops | bytes accessed | tf_op | source)
XLA Modules:
  0.0 92.6 jit_solution(15930509631723306382)
XLA Ops:
  0.0 1.3 %bitcast_bitcast_fusion = f32[2,8,32,2,128]{4,3,2,1,0:T(2,128)S(1)} fusion(f32[8,32,2,512]{3,2,1,0:T(2,128)} %param.12, s32[]{:T(128)S(6)} %select_n.18, pred[]{:T(512)S(6)} %eq.3), kind=kLoop, calls=%fused_computation | loop fusion | flops 131072 | bytes 1048581 | tf_op jit(solution)/shard_map/jit(_where)/select_n | solution.py:1039
  1.3 1.2 %reshape.24.begin = f32[2,8,32,256]{3,2,1,0:T(8,128)} reshape(f32[2,8,32,2,128]{4,3,2,1,0:T(2,128)S(1)} %bitcast_bitcast_fusion) | data formatting | bytes 1048576 | tf_op jit(solution)/shard_map/reshape | solution.py:1039
  2.5 87.7 %shard_map.73 = bf16[4,8,32,512]{3,2,1,0:T(8,128)(2,1)} custom-call(bf16[2,4,32,4608]{3,2,1,0:T(8,128)(2,1)} %bitcast.12, bf16[3,3,2,4,32,512]{5,4,3,2,1,0:T(8,128)(2,1)} %bitcast.13, bf16[4,8,32,512]{3,2,1,0:T(8,128)(2,1)} %frames.1, f32[2,8,32,256]{3,2,1,0:T(8,128)} %reshape.24.begin, f32[4,128]{1,0:T(4,128)} %bitcast.14, f32[4,128]{1,0:T(4,128)} %bitcast.15, ...), custom_call_target="tpu_custom_call" | custom-call | tf_op jit(solution)/shard_map/pallas_call | solution.py:995
  90.2 2.3 %copy.12 = bf16[4,8,32,512]{3,2,1,0:T(8,128)(2,1)} copy(bf16[4,8,32,512]{3,2,1,0:T(8,128)(2,1)} %shard_map.73) | data formatting | bytes 2097152

commit v2 on v1

--- a/solution.py
+++ b/solution.py
@@ -380,8 +380,8 @@
 
 
 def layer_kernel(
-    win, wout, frames, begin, rate, angle, skip, out,
-    views, full_in, full_out, driven, held, acc, tail, tail_half, met, joint, far_joint, given, got,
+    win, wout, frames, start, rate, angle, skip, out,
+    started, begin, views, full_in, full_out, driven, held, acc, tail, tail_half, met, joint, far_joint, given, got,
     z_send, z_recv, x_send, x_recv, y_send, y_recv,
     halo_send, halo_recv, pass_send, pass_recv, edge_send, edge_recv,
     first_send, first_recv, second_send, second_recv, swap_send, swap_recv, part_send, part_recv, local,
@@ -396,9 +396,9 @@
     band, mine = padded - 2, many // 2
     lanes = tail.shape[-1] // 2
     depth = 3 * channels
-    own = row // 2 == core
-    near = jnp.where(row <= 2 * core, 0, 1)
+    near = row // 2
     slots = (near, 1 - near)
+    turns = (row + 1 - 2 * (row % 2), 2 - near, 3 * (1 - near))
     here = pl.multiple_of(core * mine, mine)
     there = pl.multiple_of(other * mine, mine)
     has_up, has_down = row > 0, row < rows - 1
@@ -409,157 +409,151 @@
             device_id=where, device_id_type=pl.DeviceIdType.MESH,
         )
 
-    def block(w, slot, quarter, o):
-        a = ORDER[o]
+    def block(w, shard, quarter, o):
+        a, pair, j = ORDER[o], shard // 2, shard % 2
         if w == 0:
-            return full_in.at[slot, :, quarter, :, a * depth : (a + 1) * depth]
-        return full_out.at[a, :, slot, :, quarter]
+            return full_in.at[pair, :, j, quarter, :, a * depth : (a + 1) * depth]
+        return full_out.at[a, :, pair, :, j, quarter]
 
     def source(w, quarter, o):
         a = ORDER[o]
         if w == 0:
-            return win.at[:, quarter, :, a * depth : (a + 1) * depth]
-        return wout.at[a, :, :, quarter]
-
-    def z_piece(k):
-        return (chip, k) if k < 3 else (opposite, 2)
-
-    def z_copy(w, slot, k, kind, first, to):
-        quarter, o = z_piece(k)
-        dst = block(w, slot, quarter, o)
+            return win.at[:, core, quarter, :, a * depth : (a + 1) * depth]
+        return wout.at[a, :, :, core, quarter]
+
+    def z_copy(w, shard, k, kind, first, to):
+        quarter, o = (chip, k) if k < 3 else (opposite, 2)
+        dst = block(w, shard, quarter, o)
         src = source(w, quarter, o) if first else dst
-        return remote(src, dst, z_send.at[w, kind, k], z_recv.at[w, slot, k], **{ROWS: to})
-
-    def x_copy(w, rank, i):
+        return remote(src, dst, z_send.at[w, kind, k], z_recv.at[w, shard, k], **{ROWS: to})
+
+    def x_copy(w, turn, i):
         quarter, o = (chip, i) if i < 3 else (across, 1)
-        ref = block(w, slots[rank], quarter, o)
-        return remote(ref, ref, x_send.at[w, rank, i], x_recv.at[w, rank, i], **{CHIPS: beside})
-
-    def y_copy(w, rank, i):
+        ref = block(w, turns[turn], quarter, o)
+        return remote(ref, ref, x_send.at[w, turn, i], x_recv.at[w, turn, i], **{CHIPS: beside})
+
+    def y_copy(w, turn, i):
         quarter, o = (chip, i) if i < 3 else (beside, 0)
-        ref = block(w, slots[rank], quarter, o)
-        return remote(ref, ref, y_send.at[w, rank, i], y_recv.at[w, rank, i], **{CHIPS: across})
-
-    def x_came(w, rank, i):
+        ref = block(w, turns[turn], quarter, o)
+        return remote(ref, ref, y_send.at[w, turn, i], y_recv.at[w, turn, i], **{CHIPS: across})
+
+    def x_came(w, turn, i):
         quarter, o = (beside, i) if i < 3 else (opposite, 1)
-        ref = block(w, slots[rank], quarter, o)
-        remote(ref, ref, x_send.at[w, rank, i], x_recv.at[w, rank, i], **{CHIPS: beside}).wait_recv()
-
-    def y_came(w, rank, i):
+        ref = block(w, turns[turn], quarter, o)
+        remote(ref, ref, x_send.at[w, turn, i], x_recv.at[w, turn, i], **{CHIPS: beside}).wait_recv()
+
+    def y_came(w, turn, i):
         quarter, o = (across, i) if i < 3 else (opposite, 0)
-        ref = block(w, slots[rank], quarter, o)
-        remote(ref, ref, y_send.at[w, rank, i], y_recv.at[w, rank, i], **{CHIPS: across}).wait_recv()
-
-    def apart(rank):
-        return jnp.logical_not(own) if rank == 0 else jnp.logical_or(own, True)
-
-    def from_below(rank):
-        return 2 * core + slots[rank] > row
-
-    def relays(rank):
-        below = from_below(rank)
-        return (
-            jnp.logical_and(apart(rank), jnp.logical_and(below, has_up)),
-            jnp.logical_and(apart(rank), jnp.logical_and(jnp.logical_not(below), has_down)),
+        ref = block(w, turns[turn], quarter, o)
+        remote(ref, ref, y_send.at[w, turn, i], y_recv.at[w, turn, i], **{CHIPS: across}).wait_recv()
+
+    def relays(turn):
+        below = turns[turn] > row
+        return jnp.logical_and(below, has_up), jnp.logical_and(jnp.logical_not(below), has_down)
+
+    inner = jnp.logical_and(has_up, has_down)
+    mate_up = row % 2 == 1
+    early_up = jnp.logical_and(has_up, jnp.logical_or(jnp.logical_not(inner), jnp.logical_not(mate_up)))
+    early_down = jnp.logical_and(has_down, jnp.logical_or(jnp.logical_not(inner), mate_up))
+
+    def send_own(w, ks, up=has_up, down=has_down):
+        for k in ks:
+            @pl.when(up)
+            def _():
+                z_copy(w, row, k, 3, True, row - 1).start()
+
+            @pl.when(down)
+            def _():
+                z_copy(w, row, k, 4, True, row + 1).start()
+
+    late_up = jnp.logical_and(has_up, jnp.logical_not(early_up))
+    late_down = jnp.logical_and(has_down, jnp.logical_not(early_down))
+
+    def send_early(w):
+        send_own(w, range(4), early_up, early_down)
+
+    def send_late(w, which):
+        send_own(
+            w, range(4), jnp.logical_and(late_up, core == which), jnp.logical_and(late_down, core == which)
         )
 
-    def guarded(rank, do):
-        if rank == 0:
-            pl.when(apart(0))(do)
+    def bring(w, turn, k):
+        shard = turns[turn]
+        z_copy(w, shard, k, turn, False, row).wait_recv()
+        up, down = relays(turn)
+
+        @pl.when(up)
+        def _():
+            z_copy(w, shard, k, turn, False, row - 1).start()
+
+        @pl.when(down)
+        def _():
+            z_copy(w, shard, k, turn, False, row + 1).start()
+
+    def fan(w, turn, k, x=True, y=True):
+        if x:
+            x_copy(w, turn, k).start()
+        if y:
+            y_copy(w, turn, k).start()
+
+    def z_event(w, turn, k):
+        bring(w, turn, k)
+        if k < 3:
+            fan(w, turn, k)
+
+    def x_event(w, turn):
+        x_came(w, turn, 0)
+        y_copy(w, turn, 3).start()
+
+    def y_event(w, turn):
+        y_came(w, turn, 1)
+        x_copy(w, turn, 3).start()
+
+    def events(w, turn):
+        return [
+            functools.partial(z_event, w, turn, 0),
+            functools.partial(z_event, w, turn, 1),
+            functools.partial(x_event, w, turn),
+            functools.partial(z_event, w, turn, 2),
+            functools.partial(y_event, w, turn),
+            functools.partial(z_event, w, turn, 3),
+        ]
+
+    def came(w, turn, o):
+        if o != 0:
+            x_came(w, turn, o)
         else:
-            do()
-
-    def send_own(w):
-        for k in range(4):
-            @pl.when(jnp.logical_and(own, has_up))
-            def _():
-                z_copy(w, near, k, 0, True, row - 1).start()
-
-            @pl.when(jnp.logical_and(own, has_down))
-            def _():
-                z_copy(w, near, k, 2, True, row + 1).start()
-
-    def z_event(w, rank, k):
-        slot = slots[rank]
-
-        def do():
-            z_copy(w, slot, k, rank, False, row).wait_recv()
-            if k < 3:
-                x_copy(w, rank, k).start()
-                y_copy(w, rank, k).start()
-
-        guarded(rank, do)
-        up, down = relays(rank)
-
-        @pl.when(up)
-        def _():
-            z_copy(w, slot, k, rank, False, row - 1).start()
-
-        @pl.when(down)
-        def _():
-            z_copy(w, slot, k, rank, False, row + 1).start()
-
-    def x_event(w, rank):
-        def do():
-            x_came(w, rank, 0)
-            y_copy(w, rank, 3).start()
-
-        guarded(rank, do)
-
-    def y_event(w, rank):
-        def do():
-            y_came(w, rank, 1)
-            x_copy(w, rank, 3).start()
-
-        guarded(rank, do)
-
-    def events(w, rank):
-        return [
-            functools.partial(z_event, w, rank, 0),
-            functools.partial(z_event, w, rank, 1),
-            functools.partial(x_event, w, rank),
-            functools.partial(z_event, w, rank, 2),
-            functools.partial(y_event, w, rank),
-            functools.partial(z_event, w, rank, 3),
-        ]
+            y_came(w, turn, 3)
+        if o != 1:
+            y_came(w, turn, o)
+        else:
+            x_came(w, turn, 3)
 
     def complete(w, rank, o):
-        def do():
-            if o != 0:
-                x_came(w, rank, o)
-            else:
-                y_came(w, rank, 3)
-            if o != 1:
-                y_came(w, rank, o)
-            else:
-                x_came(w, rank, 3)
-
-        guarded(rank, do)
+        for turn in ((1, 2) if rank else (0,)):
+            came(w, turn, o)
 
     def settle(w):
         for k in range(4):
-            @pl.when(jnp.logical_and(own, has_up))
+            @pl.when(has_up)
             def _():
-                z_copy(w, near, k, 0, True, row - 1).wait_send()
-
-            @pl.when(jnp.logical_and(own, has_down))
+                z_copy(w, row, k, 3, True, row - 1).wait_send()
+
+            @pl.when(has_down)
             def _():
-                z_copy(w, near, k, 2, True, row + 1).wait_send()
-
-            for rank in range(2):
-                up, down = relays(rank)
+                z_copy(w, row, k, 4, True, row + 1).wait_send()
+
+            for turn in range(3):
+                up, down = relays(turn)
 
                 @pl.when(jnp.logical_or(up, down))
                 def _():
-                    z_copy(w, slots[rank], k, rank, False, row).wait_send()
-
-        for rank in range(2):
-            def do():
-                for i in range(4):
-                    x_copy(w, rank, i).wait_send()
-                    y_copy(w, rank, i).wait_send()
-
-            guarded(rank, do)
+                    z_copy(w, turns[turn], k, turn, False, row).wait_send()
+
+        for turn in range(3):
+            for i in range(4):
+                x_copy(w, turn, i).wait_send()
+                y_copy(w, turn, i).wait_send()
 
     barrier = pltpu.get_barrier_semaphore()
 
@@ -582,8 +576,9 @@
 
     mine_in = views.at[1, pl.ds(here, mine), 1 : band + 1]
     keep = pltpu.make_async_copy(frames, mine_in, local.at[0])
-    hold_in = pltpu.make_async_copy(win, full_in.at[near], local.at[1])
-    hold_out = pltpu.make_async_copy(wout, full_out.at[:, :, near], local.at[2])
+    hold_in = pltpu.make_async_copy(win.at[:, core], full_in.at[near, :, row % 2], local.at[1])
+    hold_out = pltpu.make_async_copy(wout.at[:, :, :, core], full_out.at[:, :, near, :, row % 2], local.at[2])
+    hold_start = pltpu.make_async_copy(start, started, local.at[3])
     swap = remote(frames, mine_in, swap_send, swap_recv, **{CORE: other})
     theirs_in = views.at[1, pl.ds(there, mine), 1 : band + 1]
 
@@ -606,19 +601,21 @@
     gives = (has_up, has_down)
     takes = (has_down, has_up)
 
+    send_own(0, range(4))
+    for side in range(2):
+        @pl.when(gives[side])
+        def _():
+            halo(side, True).start()
+
     swap.start()
     keep.start()
-    for side in range(2):
-        @pl.when(gives[side])
-        def _():
-            halo(side, True).start()
-
-    send_own(0)
-
-    @pl.when(own)
+
+    hold_in.start()
+    hold_out.start()
+
+    @pl.when(chip == 0)
     def _():
-        hold_in.start()
-        hold_out.start()
+        hold_start.start()
 
     blank = jnp.zeros((columns, channels), views.dtype)
     for side in range(2):
@@ -640,14 +637,38 @@
         after = jnp.where(not_last, pltpu.roll(wide, columns - 1, 0), 0.0)
         return before.astype(views.dtype), after.astype(views.dtype)
 
-    def spread_views(first, count):
-        @pl.loop(0, count)
+    def spread_views(first):
+        @pl.loop(0, mine)
         def _(i):
             f = first + i
 
-            @pl.loop(0, padded)
+            @pl.loop(1, band + 1)
             def _(r):
                 views[0, f, r], views[2, f, r] = sides(views[1, f, r].astype(jnp.float32))
+
+    def spread_edges(first):
+        @pl.loop(0, mine)
+        def _(i):
+            f = first + i
+            for r in (0, band + 1):
+                views[0, f, r], views[2, f, r] = sides(views[1, f, r].astype(jnp.float32))
+
+    def hand_over():
+        for side in range(2):
+            @pl.when(takes[side])
+            def _():
+                halo_came(side)
+                handed(side, here).start()
+
+        spread_edges(here)
+
+    def take_over():
+        for side in range(2):
+            @pl.when(takes[side])
+            def _():
+                handed(side, there).wait_recv()
+
+        spread_edges(there)
 
     def drive(rank, o, m0, m1):
         slot, a = slots[rank], ORDER[o]
@@ -659,7 +680,7 @@
             window = jnp.concatenate(
                 [views[b, at, a : a + band].reshape(pixels, channels) for b in range(3)], axis=1
             )
-            weight = full_in[slot, :, :, :, a * depth : (a + 1) * depth].reshape(2 * lanes, depth)
+            weight = full_in[slot, :, :, :, :, a * depth : (a + 1) * depth].reshape(2 * lanes, depth)
             result = lax.dot_general(
                 window, weight, (((1,), (1,)), ((), ())), preferred_element_type=jnp.float32
             ).reshape(2, band, columns, 2 * lanes)
@@ -670,10 +691,43 @@
 
     blocks = many // 2
 
+    low = lax.broadcasted_iota(jnp.int32, (1, lanes), 1) < lanes // 2
+
+    def joined(first, second):
+        first = jnp.where(core == 0, first, pltpu.roll(first, lanes // 2, 1))
+        second = jnp.where(core == 0, pltpu.roll(second, lanes // 2, 1), second)
+        return jnp.where(low, first, second)
+
     def factors(rank):
-        at = pl.ds(2 * core + slots[rank], 1)
-        modulus = jnp.exp(-rate[at, :])
-        return modulus * jnp.cos(angle[at, :]), modulus * jnp.sin(angle[at, :])
+        def lane_row(ref):
+            first, second = (
+                jnp.broadcast_to(ref[pl.ds(2 * slots[rank] + j, 1), :], (8, lanes)) for j in range(2)
+            )
+            return joined(first, second)[:1]
+
+        modulus, turn = jnp.exp(-lane_row(rate)), lane_row(angle)
+        return modulus * jnp.cos(turn), modulus * jnp.sin(turn)
+
+    def prepare():
+        @pl.when(chip == 0)
+        def _():
+            hold_start.wait()
+
+            @pl.loop(0, band)
+            def _(r):
+                for pair in range(2):
+                    for part in range(2):
+                        at = slice(part * lanes, (part + 1) * lanes)
+                        begin[pair, r, :, at] = joined(
+                            started[r, :, 4 * pair + part], started[r, :, 4 * pair + 2 + part]
+                        )
+
+        @pl.when(chip > 0)
+        def _():
+            @pl.loop(0, band)
+            def _(r):
+                for pair in range(2):
+                    begin[pair, r] = jnp.zeros((columns, 2 * lanes), jnp.float32)
 
     def ends(rank):
         slot = slots[rank]
@@ -849,8 +903,8 @@
             return result
         return acc[pl.ds(first, 2)] + result
 
-    def mix(rank, rights, fresh):
-        @pl.loop(0, blocks)
+    def mix(rank, rights, fresh, m0=0, m1=None):
+        @pl.loop(m0, blocks if m1 is None else m1)
         def _(m):
             acc[pl.ds(m * 2, 2)] = mix_block(rank, rights, m * 2, fresh)
 
@@ -881,81 +935,185 @@
 
     steps = iter(events(0, 0))
     next(steps)()
+    next(steps)()
     keep.wait()
-    for side in range(2):
-        @pl.when(takes[side])
-        def _():
-            halo_came(side)
-            handed(side, here).start()
-
+    spread_views(here)
     next(steps)()
-    spread_views(here, mine // 2)
     next(steps)()
-    spread_views(here + mine // 2, mine // 2)
+    prepare()
+    next(steps)()
     next(steps)()
     remote(theirs_in, theirs_in, swap_send, swap_recv, **{CORE: other}).wait_recv()
-    for side in range(2):
-        @pl.when(takes[side])
-        def _():
-            handed(side, there).wait_recv()
-
-    spread_views(there, mine // 2)
-    next(steps)()
-    spread_views(there + mine // 2, mine // 2)
-    next(steps)()
-
-    @pl.when(own)
+    spread_views(there)
+    hand_over()
+    hold_in.wait()
+    hold_out.wait()
+    half = blocks // 2
+
+    @pl.when(inner)
     def _():
-        hold_in.wait()
-        hold_out.wait()
-
-    steps = iter(events(0, 1))
-    for o in range(3):
-        next(steps)()
-        complete(0, 0, o)
-        drive(0, o, 0, blocks // 2)
-        next(steps)()
-        drive(0, o, blocks // 2, blocks)
-    send_own(1)
-    ends(0)
-    tell(0)
-    steps = iter(events(1, 0))
-    complete(0, 1, 0)
-    drive(1, 0, 0, blocks)
-    next(steps)()
-    complete(0, 1, 1)
-    merge(0)
-    drive(1, 1, 0, blocks)
-    next(steps)()
-    complete(0, 1, 2)
-    drive(1, 2, 0, blocks)
-    ends(1)
-    tell(1)
-    for step in steps:
-        step()
-    carry(0)
-    scan(0)
-    merge(1)
-    steps = iter(events(1, 1))
-    next(steps)()
-    next(steps)()
-    complete(1, 0, 0)
-    mix(0, (1,), True)
-    carry(1)
-    scan(1)
-    for step in steps:
-        step()
-    edges_came(0)
-    complete(1, 0, 1)
-    complete(1, 0, 2)
-    mix(0, (0, 2), False)
-    complete(1, 1, 0)
-    mix(1, (1,), False)
-    edges_came(1)
-    complete(1, 1, 1)
-    complete(1, 1, 2)
-    mix_last(1, (0, 2))
-
+        z_event(0, 1, 0)
+        z_event(0, 1, 1)
+        complete(0, 0, 0)
+        drive(0, 0, 0, half)
+        z_event(0, 1, 2)
+        z_event(0, 1, 3)
+        drive(0, 0, half, blocks)
+        z_event(0, 2, 0)
+        x_event(0, 1)
+        take_over()
+        complete(0, 0, 1)
+        drive(0, 1, 0, half)
+        z_event(0, 2, 1)
+        y_event(0, 1)
+        drive(0, 1, half, blocks)
+        z_event(0, 2, 2)
+        z_event(0, 2, 3)
+        send_early(1)
+        send_late(1, 0)
+        complete(0, 0, 2)
+        drive(0, 2, 0, blocks)
+        ends(0)
+        tell(0)
+        x_event(0, 2)
+        y_event(0, 2)
+        complete(0, 1, 0)
+        drive(1, 0, 0, blocks)
+        send_late(1, 1)
+        bring(1, 0, 0)
+        bring(1, 0, 1)
+        complete(0, 1, 1)
+        merge(0)
+        drive(1, 1, 0, blocks)
+        bring(1, 0, 2)
+        bring(1, 0, 3)
+        fan(1, 0, 0)
+        complete(0, 1, 2)
+        drive(1, 2, 0, blocks)
+        ends(1)
+        tell(1)
+        bring(1, 1, 0)
+        bring(1, 1, 1)
+        bring(1, 1, 2)
+        bring(1, 1, 3)
+        fan(1, 0, 1)
+        carry(0)
+        scan(0)
+        bring(1, 2, 0)
+        bring(1, 2, 1)
+        merge(1)
+        fan(1, 0, 2)
+        x_event(1, 0)
+        fan(1, 1, 0)
+        y_event(1, 0)
+        fan(1, 1, 1)
+        bring(1, 2, 2)
+        bring(1, 2, 3)
+        fan(1, 1, 2)
+        carry(1)
+        scan(1)
+        complete(1, 0, 0)
+        mix(0, (1,), True)
+        x_event(1, 1)
+        fan(1, 2, 0)
+        edges_came(0)
+        complete(1, 0, 1)
+        mix(0, (0,), False)
+        y_event(1, 1)
+        fan(1, 2, 1)
+        fan(1, 2, 2)
+        complete(1, 0, 2)
+        mix(0, (2,), False)
+        x_event(1, 2)
+        y_event(1, 2)
+        edges_came(1)
+        complete(1, 1, 2)
+        mix(1, (2,), False)
+        complete(1, 1, 0)
+        mix(1, (1,), False)
+        complete(1, 1, 1)
+
+    @pl.when(jnp.logical_not(inner))
+    def _():
+        z_event(0, 1, 0)
+        complete(0, 0, 0)
+        drive(0, 0, 0, half)
+        z_event(0, 1, 1)
+        drive(0, 0, half, blocks)
+        x_event(0, 1)
+        take_over()
+        complete(0, 0, 1)
+        drive(0, 1, 0, half)
+        z_event(0, 1, 2)
+        send_early(1)
+        drive(0, 1, half, blocks)
+        y_event(0, 1)
+        z_event(0, 1, 3)
+        complete(0, 0, 2)
+        drive(0, 2, 0, half)
+        z_event(0, 2, 0)
+        drive(0, 2, half, blocks)
+        z_event(0, 2, 1)
+        ends(0)
+        tell(0)
+        x_event(0, 2)
+        z_event(0, 2, 2)
+        y_event(0, 2)
+        complete(0, 1, 0)
+        drive(1, 0, 0, blocks)
+        z_event(0, 2, 3)
+        complete(0, 1, 1)
+        merge(0)
+        drive(1, 1, 0, blocks)
+        bring(1, 0, 0)
+        fan(1, 0, 0)
+        complete(0, 1, 2)
+        drive(1, 2, 0, blocks)
+        ends(1)
+        tell(1)
+        bring(1, 0, 1)
+        fan(1, 0, 1)
+        carry(0)
+        scan(0)
+        bring(1, 0, 2)
+        fan(1, 0, 2, x=False)
+        merge(1)
+        fan(1, 0, 2, y=False)
+        x_event(1, 0)
+        bring(1, 0, 3)
+        z_event(1, 1, 0)
+        y_event(1, 0)
+        z_event(1, 1, 1)
+        carry(1)
+        scan(1)
+        z_event(1, 1, 2)
+        complete(1, 0, 0)
+        mix(0, (1,), True, 0, half)
+        x_event(1, 1)
+        mix(0, (1,), True, half)
+        z_event(1, 1, 3)
+        z_event(1, 2, 0)
+        edges_came(0)
+        complete(1, 0, 1)
+        mix(0, (0,), False, 0, half)
+        z_event(1, 2, 1)
+        y_event(1, 1)
+        mix(0, (0,), False, half)
+        z_event(1, 2, 2)
+        complete(1, 0, 2)
+        mix(0, (2,), False, 0, half)
+        x_event(1, 2)
+        mix(0, (2,), False, half)
+        z_event(1, 2, 3)
+        y_event(1, 2)
+        edges_came(1)
+        complete(1, 1, 2)
+        mix(1, (2,), False)
+        complete(1, 1, 0)
+        mix(1, (1,), False)
+        complete(1, 1, 1)
+
+    mix_last(1, (0,))
     settle(0)
     settle(1)
     swap.wait_send()
@@ -986,7 +1144,7 @@
 def layer(weight_in, weight_out, frames_in, start, log_decay, rotation, skip_gain):
     count, band, columns, channels = frames_in.shape
     lanes = weight_in.shape[1]
-    quarter = lanes // 4
+    quarter = lanes // 8
     many = 2 * count
     vmem, anywhere = pl.BlockSpec(memory_space=pltpu.VMEM), pl.BlockSpec(memory_space=pl.ANY)
     dma = pltpu.SemaphoreType.DMA
@@ -995,12 +1153,14 @@
     return pl.pallas_call(
         layer_kernel,
         out_shape=jax.ShapeDtypeStruct(frames_in.shape, half),
-        in_specs=[anywhere, anywhere, anywhere, vmem, vmem, vmem, vmem],
+        in_specs=[anywhere, anywhere, anywhere, anywhere, vmem, vmem, vmem],
         out_specs=vmem,
         scratch_shapes=[
+            pltpu.VMEM(start.shape, full),
+            pltpu.VMEM((2, band, columns, 2 * lanes), full),
             pltpu.VMEM((3, many, band + 2, columns, channels), half),
-            pltpu.VMEM((2, 2, 4, quarter, 9 * channels), half),
-            pltpu.VMEM((3, 3, 2, 2, 4, quarter, channels), half),
+            pltpu.VMEM((2, 2, 2, 4, quarter, 9 * channels), half),
+            pltpu.VMEM((3, 3, 2, 2, 2, 4, quarter, channels), half),
             pltpu.VMEM((2, many, band, columns, 2 * lanes), full),
             pltpu.VMEM((2, 3, many, band + 2, columns, 2 * lanes), half),
             pltpu.VMEM((many, band, columns, channels), full),
@@ -1011,17 +1171,17 @@
             pltpu.VMEM((2, band, columns, 2 * lanes), half),
             pltpu.VMEM((count, band, columns, channels), half),
             pltpu.VMEM((count, band, columns, channels), half),
-            dma((2, 3, 4)), dma((2, 2, 4)), dma((2, 2, 4)), dma((2, 2, 4)), dma((2, 2, 4)), dma((2, 2, 4)),
+            dma((2, 5, 4)), dma((2, 4, 4)), dma((2, 3, 4)), dma((2, 3, 4)), dma((2, 3, 4)), dma((2, 3, 4)),
             dma((2,)), dma((2,)), dma((2,)), dma((2,)), dma((2, 2)), dma((2, 2)),
             dma((2,)), dma((2,)), dma((2,)), dma((2,)), dma, dma,
-            dma((many // 4,)), dma((many // 4,)), dma((3,)),
+            dma((many // 4,)), dma((many // 4,)), dma((4,)),
         ],
         compiler_params=pltpu.CompilerParams(
             collective_id=3, has_side_effects=True, vmem_limit_bytes=63 * 1024 * 1024
         ),
     )(
-        weight_in.reshape(2, 4, quarter, 9 * channels),
-        weight_out.reshape(3, 3, 2, 4, quarter, channels),
+        weight_in.reshape(2, 2, 4, quarter, 9 * channels),
+        weight_out.reshape(3, 3, 2, 2, 4, quarter, channels),
         frames_in,
         start,
         log_decay.reshape(-1, lanes),
@@ -1031,12 +1191,9 @@
 
 
 def fused(frames_in, weight_in, weight_out, log_decay, rotation, start_state, skip_gain):
-    core, chip = lax.axis_index(CORE), lax.axis_index(CHIPS)
     lanes = weight_in.shape[1]
     band, columns = start_state.shape[:2]
-    start = lax.dynamic_slice_in_dim(start_state, core * 2 * lanes, 2 * lanes, 3)
-    start = start.reshape(band, columns, 2, 2, lanes).transpose(3, 0, 1, 2, 4)
-    start = jnp.where(chip == 0, start, jnp.float32(0.0)).reshape(2, band, columns, 2 * lanes)
+    start = start_state.reshape(band, columns, 2, -1, lanes).swapaxes(2, 3).reshape(band, columns, -1, lanes)
     return layer(weight_in, weight_out, frames_in, start, log_decay, rotation, skip_gain)
 
 

time: 92.8 us -> 87.9 us (0.947); the launches traced: 92.6 us -> 86.4 us
  Pallas kernels: 87.7 us -> 84.1 us
  other arithmetic: 1.31 us -> 0 us
  local copies, waits for them, and re-layouts: 3.52 us -> 2.3 us
    pallas_call x1, Pallas kernels: 87.7 us -> 84.1 us  [layer(): pl.pallas_call(layer_kernel, out_shape=jax.ShapeDtypeStruct(frames_in.sha...]
    select_n x1 -> x0, other arithmetic: 1.31 us -> none  [fused(): jnp.where(chip == 0, start, jnp.float32(0.0))]
    reshape x1 -> x0, local copies, waits for them, and re-layouts: 1.22 us -> none  [fused(): jnp.where(chip == 0, start, jnp.float32(0.0))]
where the time goes in v2:
time: 87.9 us; the launch traced here: 86.4 us
  Pallas kernels  84.1 us (96%)
  local copies, waits for them, and re-layouts  2.3 us (3%)
    pallas_call x1, Pallas kernels, layer(): pl.pallas_call(layer_kernel, out_shape=jax.ShapeDtypeStruct(frames_in.sha...  84.1 us
    unnamed x1, local copies, waits for them, and re-layouts  2.3 us

profile of v2, /device:TPU:5, one launch (start us, length us, event | category | flops | bytes accessed | tf_op | source)
XLA Modules:
  0.0 86.4 jit_solution(477573481389399228)
XLA Ops:
  0.0 84.1 %shard_map.73 = bf16[4,8,32,512]{3,2,1,0:T(8,128)(2,1)} custom-call(bf16[2,2,4,16,4608]{4,3,2,1,0:T(8,128)(2,1)} %bitcast.10, bf16[3,3,2,2,4,16,512]{6,5,4,3,2,1,0:T(8,128)(2,1)} %bitcast.11, bf16[4,8,32,512]{3,2,1,0:T(8,128)(2,1)} %frames.1, f32[8,32,8,128]{3,2,1,0:T(8,128)} %bitcast.12, f32[4,128]{1,0:T(4,128)} %bitcast.13, f32[4,128]{1,0:T(4,128)} %bitcast.14, ...), custom_call_target="tpu_custom_call" | custom-call | tf_op jit(solution)/shard_map/pallas_call | solution.py:1153
  84.1 2.3 %copy.10 = bf16[4,8,32,512]{3,2,1,0:T(8,128)(2,1)} copy(bf16[4,8,32,512]{3,2,1,0:T(8,128)(2,1)} %shard_map.73) | data formatting | bytes 2097152

commit v3 on v2

--- a/solution.py
+++ b/solution.py
@@ -380,11 +380,11 @@
 
 
 def layer_kernel(
-    win, wout, frames, start, rate, angle, skip, out,
-    started, begin, views, full_in, full_out, driven, held, acc, tail, tail_half, met, joint, far_joint, given, got,
+    win, wout, frames, start, rate_in, angle_in, skip_in, out,
+    rate, angle, skip, done, started, begin, views, full_in, full_out, driven, held, acc, tail, tail_half, met, joint, far_joint, given, got,
     z_send, z_recv, x_send, x_recv, y_send, y_recv,
     halo_send, halo_recv, pass_send, pass_recv, edge_send, edge_recv,
-    first_send, first_recv, second_send, second_recv, swap_send, swap_recv, part_send, part_recv, local,
+    first_send, first_recv, second_send, second_recv, swap_send, swap_recv, part_send, part_recv, local, out_sem,
 ):
     chip, core, row = (lax.axis_index(a) for a in (CHIPS, CORE, ROWS))
     rows = lax.axis_size(ROWS)
@@ -602,14 +602,21 @@
     takes = (has_down, has_up)
 
     send_own(0, range(4))
+    held_back = (jnp.logical_and(inner, mate_up), jnp.logical_and(inner, jnp.logical_not(mate_up)))
     for side in range(2):
-        @pl.when(gives[side])
+        @pl.when(jnp.logical_and(gives[side], jnp.logical_not(held_back[side])))
         def _():
             halo(side, True).start()
 
     swap.start()
     keep.start()
 
+    small = [
+        pltpu.make_async_copy(src, dst, local.at[4 + i])
+        for i, (src, dst) in enumerate(((rate_in, rate), (angle_in, angle), (skip_in, skip)))
+    ]
+    for copy in small:
+        copy.start()
     hold_in.start()
     hold_out.start()
 
@@ -914,6 +921,9 @@
             given.at[at], got.at[at], part_send.at[m], part_recv.at[m], **{CORE: other}
         )
 
+    def out_copy(f):
+        return pltpu.make_async_copy(done.at[f], out.at[f], out_sem.at[f])
+
     def mix_last(rank, rights):
         for m in range(blocks // 2):
             given[m * 2 : m * 2 + 2] = mix_block(rank, rights, there + m * 2, False).astype(given.dtype)
@@ -931,11 +941,23 @@
                 def _(r):
                     value = acc[here + f, r] + got[f, r].astype(jnp.float32)
                     value = value + skip[...] * views[1, here + f, 1 + r].astype(jnp.float32)
-                    out[f, r] = (0.5 * value * (1.0 + lax.erf(value * 0.7071067811865476))).astype(out.dtype)
+                    done[f, r] = (0.5 * value * (1.0 + lax.erf(value * 0.7071067811865476))).astype(done.dtype)
+
+                out_copy(f).start()
 
     steps = iter(events(0, 0))
     next(steps)()
     next(steps)()
+
+    @pl.when(inner)
+    def _():
+        bring(0, 1, 0)
+        bring(0, 1, 1)
+        for side in range(2):
+            @pl.when(held_back[side])
+            def _():
+                halo(side, True).start()
+
     keep.wait()
     spread_views(here)
     next(steps)()
@@ -945,20 +967,23 @@
     next(steps)()
     remote(theirs_in, theirs_in, swap_send, swap_recv, **{CORE: other}).wait_recv()
     spread_views(there)
-    hand_over()
     hold_in.wait()
     hold_out.wait()
+    for copy in small:
+        copy.wait()
     half = blocks // 2
 
     @pl.when(inner)
     def _():
-        z_event(0, 1, 0)
-        z_event(0, 1, 1)
+        fan(0, 1, 0)
+        bring(0, 1, 2)
+        bring(0, 1, 3)
+        fan(0, 1, 1)
         complete(0, 0, 0)
         drive(0, 0, 0, half)
-        z_event(0, 1, 2)
-        z_event(0, 1, 3)
+        fan(0, 1, 2)
         drive(0, 0, half, blocks)
+        hand_over()
         z_event(0, 2, 0)
         x_event(0, 1)
         take_over()
@@ -974,20 +999,20 @@
         complete(0, 0, 2)
         drive(0, 2, 0, blocks)
         ends(0)
-        tell(0)
         x_event(0, 2)
         y_event(0, 2)
+        tell(0)
         complete(0, 1, 0)
         drive(1, 0, 0, blocks)
         send_late(1, 1)
+        bring(1, 0, 2)
+        bring(1, 0, 3)
         bring(1, 0, 0)
         bring(1, 0, 1)
         complete(0, 1, 1)
+        fan(1, 0, 0)
+        drive(1, 1, 0, blocks)
         merge(0)
-        drive(1, 1, 0, blocks)
-        bring(1, 0, 2)
-        bring(1, 0, 3)
-        fan(1, 0, 0)
         complete(0, 1, 2)
         drive(1, 2, 0, blocks)
         ends(1)
@@ -999,36 +1024,37 @@
         fan(1, 0, 1)
         carry(0)
         scan(0)
-        bring(1, 2, 0)
-        bring(1, 2, 1)
+        bring(1, 2, 2)
+        bring(1, 2, 3)
         merge(1)
         fan(1, 0, 2)
         x_event(1, 0)
         fan(1, 1, 0)
         y_event(1, 0)
         fan(1, 1, 1)
-        bring(1, 2, 2)
-        bring(1, 2, 3)
+        bring(1, 2, 0)
+        bring(1, 2, 1)
         fan(1, 1, 2)
         carry(1)
         scan(1)
         complete(1, 0, 0)
         mix(0, (1,), True)
         x_event(1, 1)
-        fan(1, 2, 0)
+        fan(1, 2, 2)
         edges_came(0)
         complete(1, 0, 1)
         mix(0, (0,), False)
         y_event(1, 1)
+        fan(1, 2, 0)
         fan(1, 2, 1)
-        fan(1, 2, 2)
         complete(1, 0, 2)
         mix(0, (2,), False)
-        x_event(1, 2)
-        y_event(1, 2)
         edges_came(1)
         complete(1, 1, 2)
-        mix(1, (2,), False)
+        mix(1, (2,), False, 0, half)
+        x_event(1, 2)
+        mix(1, (2,), False, half)
+        y_event(1, 2)
         complete(1, 1, 0)
         mix(1, (1,), False)
         complete(1, 1, 1)
@@ -1041,6 +1067,7 @@
         z_event(0, 1, 1)
         drive(0, 0, half, blocks)
         x_event(0, 1)
+        hand_over()
         take_over()
         complete(0, 0, 1)
         drive(0, 1, 0, half)
@@ -1055,24 +1082,24 @@
         drive(0, 2, half, blocks)
         z_event(0, 2, 1)
         ends(0)
-        tell(0)
         x_event(0, 2)
         z_event(0, 2, 2)
         y_event(0, 2)
+        tell(0)
         complete(0, 1, 0)
         drive(1, 0, 0, blocks)
         z_event(0, 2, 3)
-        complete(0, 1, 1)
-        merge(0)
-        drive(1, 1, 0, blocks)
         bring(1, 0, 0)
         fan(1, 0, 0)
+        complete(0, 1, 1)
+        drive(1, 1, 0, blocks)
+        merge(0)
+        bring(1, 0, 1)
+        fan(1, 0, 1)
         complete(0, 1, 2)
         drive(1, 2, 0, blocks)
         ends(1)
         tell(1)
-        bring(1, 0, 1)
-        fan(1, 0, 1)
         carry(0)
         scan(0)
         bring(1, 0, 2)
@@ -1092,23 +1119,24 @@
         x_event(1, 1)
         mix(0, (1,), True, half)
         z_event(1, 1, 3)
-        z_event(1, 2, 0)
+        z_event(1, 2, 2)
         edges_came(0)
         complete(1, 0, 1)
         mix(0, (0,), False, 0, half)
-        z_event(1, 2, 1)
+        z_event(1, 2, 3)
         y_event(1, 1)
         mix(0, (0,), False, half)
-        z_event(1, 2, 2)
+        z_event(1, 2, 0)
         complete(1, 0, 2)
         mix(0, (2,), False, 0, half)
+        z_event(1, 2, 1)
+        mix(0, (2,), False, half)
         x_event(1, 2)
-        mix(0, (2,), False, half)
-        z_event(1, 2, 3)
-        y_event(1, 2)
         edges_came(1)
         complete(1, 1, 2)
-        mix(1, (2,), False)
+        mix(1, (2,), False, 0, half)
+        y_event(1, 2)
+        mix(1, (2,), False, half)
         complete(1, 1, 0)
         mix(1, (1,), False)
         complete(1, 1, 1)
@@ -1140,22 +1168,29 @@
     for m in range(blocks // 2):
         part_copy(m).wait_send()
 
+    for f in range(mine):
+        out_copy(f).wait()
+
 
 def layer(weight_in, weight_out, frames_in, start, log_decay, rotation, skip_gain):
     count, band, columns, channels = frames_in.shape
     lanes = weight_in.shape[1]
     quarter = lanes // 8
     many = 2 * count
-    vmem, anywhere = pl.BlockSpec(memory_space=pltpu.VMEM), pl.BlockSpec(memory_space=pl.ANY)
+    anywhere = pl.BlockSpec(memory_space=pl.ANY)
     dma = pltpu.SemaphoreType.DMA
     half = frames_in.dtype
     full = jnp.float32
     return pl.pallas_call(
         layer_kernel,
         out_shape=jax.ShapeDtypeStruct(frames_in.shape, half),
-        in_specs=[anywhere, anywhere, anywhere, anywhere, vmem, vmem, vmem],
-        out_specs=vmem,
+        in_specs=[anywhere] * 7,
+        out_specs=anywhere,
         scratch_shapes=[
+            pltpu.VMEM((log_decay.size // lanes, lanes), full),
+            pltpu.VMEM((log_decay.size // lanes, lanes), full),
+            pltpu.VMEM((1, channels), full),
+            pltpu.VMEM(frames_in.shape, half),
             pltpu.VMEM(start.shape, full),
             pltpu.VMEM((2, band, columns, 2 * lanes), full),
             pltpu.VMEM((3, many, band + 2, columns, channels), half),
@@ -1174,7 +1209,7 @@
             dma((2, 5, 4)), dma((2, 4, 4)), dma((2, 3, 4)), dma((2, 3, 4)), dma((2, 3, 4)), dma((2, 3, 4)),
             dma((2,)), dma((2,)), dma((2,)), dma((2,)), dma((2, 2)), dma((2, 2)),
             dma((2,)), dma((2,)), dma((2,)), dma((2,)), dma, dma,
-            dma((many // 4,)), dma((many // 4,)), dma((4,)),
+            dma((many // 4,)), dma((many // 4,)), dma((7,)), dma((count,)),
         ],
         compiler_params=pltpu.CompilerParams(
             collective_id=3, has_side_effects=True, vmem_limit_bytes=63 * 1024 * 1024

time: 87.9 us -> 83.5 us (0.950)
  Pallas kernels: 84.1 us -> 80.5 us
    pallas_call x1, Pallas kernels: 84.1 us -> 80.5 us  [layer(): pl.pallas_call(layer_kernel, out_shape=jax.ShapeDtypeStruct(frames_in.sha...]
where the time goes in v3:
time: 83.5 us; the launch traced here: 82.8 us
  Pallas kernels  80.5 us (96%)
  local copies, waits for them, and re-layouts  2.3 us (3%)
    pallas_call x1, Pallas kernels, layer(): pl.pallas_call(layer_kernel, out_shape=jax.ShapeDtypeStruct(frames_in.sha...  80.5 us
    unnamed x1, local copies, waits for them, and re-layouts  2.3 us

profile of v3, /device:TPU:5, one launch (start us, length us, event | category | flops | bytes accessed | tf_op | source)
XLA Modules:
  0.0 82.8 jit_solution(15521552880951310366)
XLA Ops:
  0.0 80.5 %shard_map.73 = bf16[4,8,32,512]{3,2,1,0:T(8,128)(2,1)} custom-call(bf16[2,2,4,16,4608]{4,3,2,1,0:T(8,128)(2,1)} %bitcast.10, bf16[3,3,2,2,4,16,512]{6,5,4,3,2,1,0:T(8,128)(2,1)} %bitcast.11, bf16[4,8,32,512]{3,2,1,0:T(8,128)(2,1)} %frames.1, f32[8,32,8,128]{3,2,1,0:T(8,128)} %bitcast.12, f32[4,128]{1,0:T(4,128)} %bitcast.13, f32[4,128]{1,0:T(4,128)} %bitcast.14, ...), custom_call_target="tpu_custom_call" | custom-call | tf_op jit(solution)/shard_map/pallas_call | solution.py:1184
  80.5 2.3 %copy.10 = bf16[4,8,32,512]{3,2,1,0:T(8,128)(2,1)} copy(bf16[4,8,32,512]{3,2,1,0:T(8,128)(2,1)} %shard_map.73) | data formatting | bytes 2097152

commit v4 on v3

--- a/solution.py
+++ b/solution.py
@@ -1009,8 +1009,8 @@
         bring(1, 0, 3)
         bring(1, 0, 0)
         bring(1, 0, 1)
+        fan(1, 0, 0)
         complete(0, 1, 1)
-        fan(1, 0, 0)
         drive(1, 1, 0, blocks)
         merge(0)
         complete(0, 1, 2)

time: 83.5 us -> 83.5 us (level)
  no operation moved by 1% of the time
where the time goes in v4:
time: 83.5 us; the launch traced here: 82.8 us
  Pallas kernels  80.5 us (96%)
  local copies, waits for them, and re-layouts  2.3 us (3%)
    pallas_call x1, Pallas kernels, layer(): pl.pallas_call(layer_kernel, out_shape=jax.ShapeDtypeStruct(frames_in.sha...  80.5 us
    unnamed x1, local copies, waits for them, and re-layouts  2.3 us

profile of v4, /device:TPU:5, one launch (start us, length us, event | category | flops | bytes accessed | tf_op | source)
XLA Modules:
  0.0 82.8 jit_solution(2693053767130880247)
XLA Ops:
  0.0 80.5 %shard_map.73 = bf16[4,8,32,512]{3,2,1,0:T(8,128)(2,1)} custom-call(bf16[2,2,4,16,4608]{4,3,2,1,0:T(8,128)(2,1)} %bitcast.10, bf16[3,3,2,2,4,16,512]{6,5,4,3,2,1,0:T(8,128)(2,1)} %bitcast.11, bf16[4,8,32,512]{3,2,1,0:T(8,128)(2,1)} %frames.1, f32[8,32,8,128]{3,2,1,0:T(8,128)} %bitcast.12, f32[4,128]{1,0:T(4,128)} %bitcast.13, f32[4,128]{1,0:T(4,128)} %bitcast.14, ...), custom_call_target="tpu_custom_call" | custom-call | tf_op jit(solution)/shard_map/pallas_call | solution.py:1184
  80.5 2.3 %copy.10 = bf16[4,8,32,512]{3,2,1,0:T(8,128)(2,1)} copy(bf16[4,8,32,512]{3,2,1,0:T(8,128)(2,1)} %shard_map.73) | data formatting | bytes 2097152
